TPU v7x, 128 devices: a whole 4x4x4 slice. The times are simulated.
128 devices in a mesh: dp: 2 (over core), segment: 4 (over x), rows: 16 (over z, y).
Axes of the slice: x: 4, y: 4, z: 4, core: 2. Of those that a mesh axis runs over, the one named last changes fastest.
Arguments:
- images: bfloat16 [8, 32, 32, 1024], P('dp', 'rows'), may hold values from -6 to 6
- cotangent: bfloat16 [8, 32, 32, 1024], P('dp', 'rows')
- pointwise: bfloat16 [8, 1024, 1024], P('segment'), may hold values from -0.1875 to 0.1875
- depthwise: float32 [8, 9, 1024], P('segment'), may hold values from -2 to 2
- norm_gain: float32 [8, 1024], P('segment'), may hold values from 0.25 to 1.75
- norm_shift: float32 [8, 1024], P('segment'), may hold values from -1.75 to 1.75
- cell_counts: int32 [4], P('segment'), may hold values from 1 to 2, as said below
- dilations: int32 [8], P('segment'), may hold values from 1 to 2, as said below
Outputs:
- section_outputs: bfloat16 [4, 8, 32, 32, 1024], P('segment', 'dp', 'rows')
- grad_pointwise: float32 [8, 1024, 1024], P('segment', ('dp', 'rows'))
- grad_depthwise: float32 [8, 9, 1024], P('segment', None, ('dp', 'rows'))
- grad_norm: float32 [8, 2, 1024], P('segment', None, ('dp', 'rows'))
Inputs may be any that keep to these rules, and one draw needn't show every extreme that they name: `cell_counts`: some section has 2 active blocks and some section one. `dilations`: slot 0 of some section has rate 2.
All inputs are finite; a program needn't handle non-finite values.
Results may differ from a plain program's by a relative error of at most 0.014.
Values may be sent and summed in bfloat16 or wider, within the bound.
A program may use at most 64 MiB of HBM per device.

v0:
```python
import jax
import jax.numpy as jnp
from jax import lax
from jax.sharding import PartitionSpec as P

DMAX = 2
MICRO = 2
IMG = 2


EPSILON = 1e-05


def padded_2(cells, sides, width):
    for axis, dim in sides:
        count = lax.axis_size(axis)
        ends = count - 1
        head = lax.slice_in_dim(cells, 0, width, axis=dim)
        tail = lax.slice_in_dim(cells, cells.shape[dim] - width, cells.shape[dim], axis=dim)
        cells = jnp.concatenate(
            [
                lax.ppermute(tail, axis, [(i, (i + 1) % count) for i in range(ends)]),
                cells,
                lax.ppermute(head, axis, [((i + 1) % count, i) for i in range(ends)]),
            ],
            axis=dim,
        )
    return cells


def shifted(value, axis, steps):
    count = lax.axis_size(axis)
    leading, last = (max(0, -steps), min(count, count - steps))
    return lax.ppermute(value, axis, [(source, source + steps) for source in range(leading, last)])


def tap_sum(padded, kernel, dilation, sign_step, row_count, col_count):
    row_axis = padded.ndim - 3
    running = jnp.zeros(
        padded.shape[:row_axis] + (row_count, col_count, padded.shape[-1]), jnp.float32
    )
    for row_tap in range(3):
        for col_tap in range(3):
            row_anchor = DMAX + sign_step * (row_tap - 1) * dilation
            col_anchor = DMAX + sign_step * (col_tap - 1) * dilation
            window = lax.dynamic_slice_in_dim(padded, row_anchor, row_count, row_axis)
            window = lax.dynamic_slice_in_dim(window, col_anchor, col_count, row_axis + 1)
            running = running + window.astype(jnp.float32) * kernel[3 * row_tap + col_tap]
    return running


def pad_cols(tensor):
    widths = [(0, 0)] * (tensor.ndim - 2) + [(DMAX, DMAX), (0, 0)]
    return jnp.pad(tensor, widths)


def put_at(store, current, positions, enabled):
    anchor = tuple((jnp.asarray(p, jnp.int32) for p in positions)) + (jnp.int32(0),) * current.ndim
    extent = (1,) * len(positions) + current.shape
    previous = lax.dynamic_slice(store, anchor, extent).reshape(current.shape)
    fresh = jnp.where(enabled, current, previous).reshape(extent)
    return lax.dynamic_update_slice(store, fresh, anchor)


def fetch_at(store, positions):
    anchor = tuple((jnp.asarray(p, jnp.int32) for p in positions)) + (jnp.int32(0),) * (
        store.ndim - len(positions)
    )
    extent = (1,) * len(positions) + store.shape[len(positions) :]
    return lax.dynamic_slice(store, anchor, extent).reshape(store.shape[len(positions) :])


def settle(partial_value):
    return lax.optimization_barrier(partial_value.astype(jnp.bfloat16)).astype(jnp.float32)


def local(images, cotangent, pointwise, depthwise, norm_gain, norm_shift, cell_counts, dilations):
    phases = lax.axis_size("segment")
    phase_id = lax.axis_index("segment")
    row_id = lax.axis_index("rows")
    row_devs = lax.axis_size("rows")
    local_rows = images.shape[1]
    columns = images.shape[2]
    channels = images.shape[3]
    height = local_rows * row_devs
    population = IMG * height * columns
    slot_count = pointwise.shape[0]
    inputs = images.reshape(MICRO, IMG, local_rows, columns, channels)
    grads_in = cotangent.reshape(MICRO, IMG, local_rows, columns, channels)
    number = cell_counts[0]
    positions = row_id * local_rows - DMAX + jnp.arange(local_rows + 2 * DMAX, dtype=jnp.int32)
    inside = ((positions >= 0) & (positions < height))[None, :, None, None]

    def normalize(padded, center, scaling, cell_slot):
        normed = (padded.astype(jnp.float32) - center) * scaling
        pre_act = normed * norm_gain[cell_slot] + norm_shift[cell_slot]
        return jnp.where(inside, jnp.maximum(pre_act, 0.0), 0.0).astype(jnp.bfloat16)

    def forward_cell(current, cell_slot):
        wide_input = current.astype(jnp.float32)
        totals, squares = lax.psum(
            (jnp.sum(wide_input, axis=(0, 1, 2)), jnp.sum(wide_input * wide_input, axis=(0, 1, 2))),
            "rows",
        )
        rimmed = padded_2(current, (("rows", 1),), DMAX)
        center = totals / population
        spread = squares / population - center * center
        scaling = lax.rsqrt(spread + EPSILON)
        activation = normalize(rimmed, center, scaling, cell_slot)
        hidden = tap_sum(
            pad_cols(activation), depthwise[cell_slot], dilations[cell_slot], 1, local_rows, columns
        ).astype(jnp.bfloat16)
        mixed_rows = jnp.dot(
            hidden.reshape(-1, channels), pointwise[cell_slot], preferred_element_type=jnp.float32
        )
        outcome = (wide_input + mixed_rows.reshape(current.shape)).astype(jnp.bfloat16)
        return (outcome, rimmed, activation, hidden, center, scaling)

    def backward_cell(gradient, cell_slot, current, activation, center, scaling):
        dilation = dilations[cell_slot]
        grad_hidden = lax.dot_general(
            gradient.reshape(-1, channels),
            pointwise[cell_slot],
            (((1,), (1,)), ((), ())),
            preferred_element_type=jnp.float32,
        )
        grad_hidden = grad_hidden.reshape(gradient.shape).astype(jnp.bfloat16)
        rim_grad = padded_2(grad_hidden, (("rows", 1),), DMAX)
        grad_act = tap_sum(
            pad_cols(rim_grad), depthwise[cell_slot], dilation, -1, local_rows, columns
        )
        wide_input = current.astype(jnp.float32)
        normed = (wide_input - center) * scaling
        pre_act = normed * norm_gain[cell_slot] + norm_shift[cell_slot]
        grad_pre = jnp.where(pre_act > 0, grad_act, 0.0)
        part_a = jnp.sum(grad_pre, axis=(0, 1, 2))
        part_b = jnp.sum(grad_pre * normed, axis=(0, 1, 2))
        total_a, total_b = lax.psum((part_a, part_b), "rows")
        grad_input = gradient.astype(jnp.float32) + scaling * norm_gain[cell_slot] * (
            grad_pre - total_a / population - normed * total_b / population
        )
        padded_act = pad_cols(activation)
        wide_grad = grad_hidden.astype(jnp.float32)
        tap_terms = []
        for row_tap in range(3):
            for col_tap in range(3):
                row_anchor = DMAX + (row_tap - 1) * dilation
                col_anchor = DMAX + (col_tap - 1) * dilation
                window = lax.dynamic_slice_in_dim(padded_act, row_anchor, local_rows, 1)
                window = lax.dynamic_slice_in_dim(window, col_anchor, columns, 2)
                tap_terms.append(jnp.sum(window.astype(jnp.float32) * wide_grad, axis=(0, 1, 2)))
        small_terms = jnp.concatenate([jnp.stack(tap_terms), part_b[None], part_a[None]], axis=0)
        return (grad_input.astype(jnp.bfloat16), small_terms)

    tick_count = MICRO + phases - 1
    blank = jnp.zeros((IMG, local_rows, columns, channels), jnp.bfloat16)
    rim_rows = local_rows + 2 * DMAX
    store_x = jnp.zeros((MICRO, slot_count, IMG, local_rows, columns, channels), jnp.bfloat16)
    store_a = jnp.zeros((MICRO, slot_count, IMG, rim_rows, columns, channels), jnp.bfloat16)
    store_h = jnp.zeros((MICRO, slot_count, IMG, local_rows, columns, channels), jnp.bfloat16)
    store_center = jnp.zeros((MICRO, slot_count, channels), jnp.float32)
    store_scaling = jnp.zeros((MICRO, slot_count, channels), jnp.float32)
    sections = jnp.zeros((MICRO, IMG, local_rows, columns, channels), jnp.bfloat16)

    def forward_tick(step_index, state_tuple):
        outgoing, store_x, store_a, store_h, store_center, store_scaling, sections = state_tuple
        incoming = shifted(outgoing, "segment", 1)
        micro_pos = step_index - phase_id
        active_tick = (micro_pos >= 0) & (micro_pos < MICRO)
        where_at = jnp.clip(micro_pos, 0, MICRO - 1)
        initial = lax.dynamic_index_in_dim(inputs, where_at, 0, keepdims=False)
        current = jnp.where(phase_id == 0, initial, incoming)
        for cell_slot in range(slot_count):
            outcome, rimmed, activation, hidden, center, scaling = forward_cell(current, cell_slot)
            store_x = put_at(store_x, current, (where_at, cell_slot), active_tick)
            store_a = put_at(store_a, activation, (where_at, cell_slot), active_tick)
            store_h = put_at(store_h, hidden, (where_at, cell_slot), active_tick)
            store_center = put_at(store_center, center, (where_at, cell_slot), active_tick)
            store_scaling = put_at(store_scaling, scaling, (where_at, cell_slot), active_tick)
            current = jnp.where(cell_slot < number, outcome, current)
        sections = put_at(sections, current, (where_at,), active_tick)
        return (current, store_x, store_a, store_h, store_center, store_scaling, sections)

    state_tuple = lax.fori_loop(
        0,
        tick_count,
        forward_tick,
        (blank, store_x, store_a, store_h, store_center, store_scaling, sections),
    )
    _, store_x, store_a, store_h, store_center, store_scaling, sections = state_tuple
    store_g = jnp.zeros((MICRO, slot_count, IMG, local_rows, columns, channels), jnp.bfloat16)
    small_acc = jnp.zeros((slot_count, 11, channels), jnp.float32)

    def backward_tick(step_index, state_tuple):
        outgoing, store_g, small_acc = state_tuple
        incoming = shifted(outgoing, "segment", -1)
        micro_pos = step_index - (phases - 1 - phase_id)
        active_tick = (micro_pos >= 0) & (micro_pos < MICRO)
        where_at = jnp.clip(micro_pos, 0, MICRO - 1)
        final_cot = lax.dynamic_index_in_dim(grads_in, where_at, 0, keepdims=False)
        gradient = jnp.where(phase_id == phases - 1, final_cot, incoming)
        for cell_slot in reversed(range(slot_count)):
            enabled = cell_slot < number
            center = fetch_at(store_center, (where_at, cell_slot))
            scaling = fetch_at(store_scaling, (where_at, cell_slot))
            current = fetch_at(store_x, (where_at, cell_slot))
            activation = fetch_at(store_a, (where_at, cell_slot))
            grad_input, small_terms = backward_cell(
                gradient, cell_slot, current, activation, center, scaling
            )
            store_g = put_at(
                store_g,
                jnp.where(enabled, gradient, jnp.zeros_like(gradient)),
                (where_at, cell_slot),
                active_tick,
            )
            small_acc = small_acc.at[cell_slot].add(
                jnp.where(enabled & active_tick, small_terms, 0.0)
            )
            gradient = jnp.where(enabled, grad_input, gradient)
        return (gradient, store_g, small_acc)

    _, store_g, small_acc = lax.fori_loop(0, tick_count, backward_tick, (blank, store_g, small_acc))
    weight_parts = []
    for cell_slot in range(slot_count):
        hidden_rows = store_h[:, cell_slot].reshape(-1, channels)
        grad_rows = store_g[:, cell_slot].reshape(-1, channels)
        weight_parts.append(
            lax.dot_general(
                hidden_rows, grad_rows, (((0,), (0,)), ((), ())), preferred_element_type=jnp.float32
            )
        )
    weight_part = settle(jnp.stack(weight_parts))
    small_part = settle(small_acc)
    summed_w, summed_s = (
        lax.psum(weight_part.astype(jnp.bfloat16), ("dp", "rows")).astype(jnp.float32),
        lax.psum(small_part.astype(jnp.bfloat16), ("dp", "rows")).astype(jnp.float32),
    )
    share = channels // lax.axis_size(("dp", "rows"))
    anchor = lax.axis_index(("dp", "rows")) * share
    grad_weight = lax.dynamic_slice_in_dim(summed_w, anchor, share, 1)
    grad_small = lax.dynamic_slice_in_dim(summed_s, anchor, share, 2)
    section_out = sections.reshape(1, MICRO * IMG, local_rows, columns, channels)
    return (section_out, grad_weight, grad_small[:, :9], grad_small[:, 9:])


def solution(mesh):
    return jax.shard_map(
        local,
        mesh=mesh,
        in_specs=(
            P("dp", "rows", None, None),
            P("dp", "rows", None, None),
            P("segment", None, None),
            P("segment", None, None),
            P("segment", None),
            P("segment", None),
            P("segment"),
            P("segment"),
        ),
        out_specs=(
            P("segment", "dp", "rows", None, None),
            P("segment", ("dp", "rows"), None),
            P("segment", None, ("dp", "rows")),
            P("segment", None, ("dp", "rows")),
        ),
        check_vma=False,
    )
```

profile of v0, /device:TPU:1, one launch (start us, length us, event | category | flops | bytes accessed | tf_op | source)
XLA Modules:
  0.0 1466.7 jit_solution(7130101652448848113)
XLA Ops:
  18.6 563.0 %while.52 = (s32[]{:T(128)}, bf16[2,2,32,1024]{3,2,1,0:T(8,128)(2,1)S(1)}, bf16[2,2,2,2,32,1024]{5,4,3,2,1,0:T(8,128)(2,1)}, bf16[2,2,2,6,32,1024]{5,4,3,2,1,0:T...) while((s32[]{:T(128)}, ...), condition=%wide.region_9.10_spmd.clone, body=%wide.region_0.9_spmd.clone.sunk | while | flops 565852160 | bytes 74467696 | solution.py:184
  39.5 34.5 %all-reduce.14 = (f32[1024]{0:T(1024)}, f32[1024]{0:T(1024)}) all-reduce(f32[1024]{0:T(1024)S(1)} %get-tuple-element.2441, f32[1024]{0:T(1024)S(1)} %get-tuple-element.2442), channel_id=1, replica_groups=mesh['dp'=2,'segment'=4,'rows'=16] {'rows'}, use_global_device_ids=true, to_apply=%region_4.4 | all-reduce | flops 2048 | bytes 16384 | tf_op jit(solution)/shard_map/while/body/eval_jaxpr/psum | solution.py:101
  86.3 4.7 collective-permute-start.4
  92.7 29.6 %all-reduce.15 = (f32[1024]{0:T(1024)}, f32[1024]{0:T(1024)}) all-reduce(f32[1024]{0:T(1024)S(1)} %get-tuple-element.2463, f32[1024]{0:T(1024)S(1)} %get-tuple-element.2464), channel_id=1, replica_groups=mesh['dp'=2,'segment'=4,'rows'=16] {'rows'}, use_global_device_ids=true, to_apply=%region_8.8 | all-reduce | flops 2048 | bytes 16384 | tf_op jit(solution)/shard_map/while/body/eval_jaxpr/psum | solution.py:101
  150.7 4.7 collective-permute-start.2
  155.4 30.3 %all-reduce.14 = (f32[1024]{0:T(1024)}, f32[1024]{0:T(1024)}) all-reduce(f32[1024]{0:T(1024)S(1)} %get-tuple-element.2441, f32[1024]{0:T(1024)S(1)} %get-tuple-element.2442), channel_id=1, replica_groups=mesh['dp'=2,'segment'=4,'rows'=16] {'rows'}, use_global_device_ids=true, to_apply=%region_4.4 | all-reduce | flops 2048 | bytes 16384 | tf_op jit(solution)/shard_map/while/body/eval_jaxpr/psum | solution.py:101
  198.0 4.7 collective-permute-start.4
  204.4 29.6 %all-reduce.15 = (f32[1024]{0:T(1024)}, f32[1024]{0:T(1024)}) all-reduce(f32[1024]{0:T(1024)S(1)} %get-tuple-element.2463, f32[1024]{0:T(1024)S(1)} %get-tuple-element.2464), channel_id=1, replica_groups=mesh['dp'=2,'segment'=4,'rows'=16] {'rows'}, use_global_device_ids=true, to_apply=%region_8.8 | all-reduce | flops 2048 | bytes 16384 | tf_op jit(solution)/shard_map/while/body/eval_jaxpr/psum | solution.py:101
  267.7 30.3 %all-reduce.14 = (f32[1024]{0:T(1024)}, f32[1024]{0:T(1024)}) all-reduce(f32[1024]{0:T(1024)S(1)} %get-tuple-element.2441, f32[1024]{0:T(1024)S(1)} %get-tuple-element.2442), channel_id=1, replica_groups=mesh['dp'=2,'segment'=4,'rows'=16] {'rows'}, use_global_device_ids=true, to_apply=%region_4.4 | all-reduce | flops 2048 | bytes 16384 | tf_op jit(solution)/shard_map/while/body/eval_jaxpr/psum | solution.py:101
  310.4 4.7 collective-permute-start.4
  315.8 29.9 %all-reduce.15 = (f32[1024]{0:T(1024)}, f32[1024]{0:T(1024)}) all-reduce(f32[1024]{0:T(1024)S(1)} %get-tuple-element.2463, f32[1024]{0:T(1024)S(1)} %get-tuple-element.2464), channel_id=1, replica_groups=mesh['dp'=2,'segment'=4,'rows'=16] {'rows'}, use_global_device_ids=true, to_apply=%region_8.8 | all-reduce | flops 2048 | bytes 16384 | tf_op jit(solution)/shard_map/while/body/eval_jaxpr/psum | solution.py:101
  379.1 30.3 %all-reduce.14 = (f32[1024]{0:T(1024)}, f32[1024]{0:T(1024)}) all-reduce(f32[1024]{0:T(1024)S(1)} %get-tuple-element.2441, f32[1024]{0:T(1024)S(1)} %get-tuple-element.2442), channel_id=1, replica_groups=mesh['dp'=2,'segment'=4,'rows'=16] {'rows'}, use_global_device_ids=true, to_apply=%region_4.4 | all-reduce | flops 2048 | bytes 16384 | tf_op jit(solution)/shard_map/while/body/eval_jaxpr/psum | solution.py:101
  421.8 4.7 collective-permute-start.4
  427.2 29.6 %all-reduce.15 = (f32[1024]{0:T(1024)}, f32[1024]{0:T(1024)}) all-reduce(f32[1024]{0:T(1024)S(1)} %get-tuple-element.2463, f32[1024]{0:T(1024)S(1)} %get-tuple-element.2464), channel_id=1, replica_groups=mesh['dp'=2,'segment'=4,'rows'=16] {'rows'}, use_global_device_ids=true, to_apply=%region_8.8 | all-reduce | flops 2048 | bytes 16384 | tf_op jit(solution)/shard_map/while/body/eval_jaxpr/psum | solution.py:101
  485.1 4.8 collective-permute-start.2
  490.0 30.3 %all-reduce.14 = (f32[1024]{0:T(1024)}, f32[1024]{0:T(1024)}) all-reduce(f32[1024]{0:T(1024)S(1)} %get-tuple-element.2441, f32[1024]{0:T(1024)S(1)} %get-tuple-element.2442), channel_id=1, replica_groups=mesh['dp'=2,'segment'=4,'rows'=16] {'rows'}, use_global_device_ids=true, to_apply=%region_4.4 | all-reduce | flops 2048 | bytes 16384 | tf_op jit(solution)/shard_map/while/body/eval_jaxpr/psum | solution.py:101
  532.6 4.7 collective-permute-start.4
  538.1 29.7 %all-reduce.15 = (f32[1024]{0:T(1024)}, f32[1024]{0:T(1024)}) all-reduce(f32[1024]{0:T(1024)S(1)} %get-tuple-element.2463, f32[1024]{0:T(1024)S(1)} %get-tuple-element.2464), channel_id=1, replica_groups=mesh['dp'=2,'segment'=4,'rows'=16] {'rows'}, use_global_device_ids=true, to_apply=%region_8.8 | all-reduce | flops 2048 | bytes 16384 | tf_op jit(solution)/shard_map/while/body/eval_jaxpr/psum | solution.py:101
  583.4 575.1 %while.53 = (s32[]{:T(128)}, bf16[2,2,32,1024]{3,2,1,0:T(8,128)(2,1)}, bf16[2,2,2,2,32,1024]{5,4,3,2,1,0:T(8,128)(2,1)}, f32[2,11,1024]{2,1,0:T(8,128)}, pred[]{...) while((s32[]{:T(128)}, ...), condition=%wide.region_37.38_spmd.clone, body=%wide.region_10.37_spmd.clone.sunk | while | flops 568489984 | bytes 45813244 | solution.py:223
  610.0 31.5 %all-reduce.16 = (f32[1024]{0:T(1024)S(1)}, f32[1024]{0:T(1024)S(1)}) all-reduce(f32[1024]{0:T(1024)S(1)} %get-tuple-element.2532, f32[1024]{0:T(1024)S(1)} %get-tuple-element.2533), channel_id=1, replica_groups=mesh['dp'=2,'segment'=4,'rows'=16] {'rows'}, use_global_device_ids=true, to_apply=%region_14.14 | all-reduce | flops 2048 | bytes 16384 | tf_op jit(solution)/shard_map/while/body/eval_jaxpr/psum | solution.py:138
  649.8 4.7 collective-permute-start.9
  662.7 29.9 %all-reduce.17 = (f32[1024]{0:T(1024)S(1)}, f32[1024]{0:T(1024)S(1)}) all-reduce(f32[1024]{0:T(1024)S(1)} %get-tuple-element.2554, f32[1024]{0:T(1024)S(1)} %get-tuple-element.2555), channel_id=1, replica_groups=mesh['dp'=2,'segment'=4,'rows'=16] {'rows'}, use_global_device_ids=true, to_apply=%region_18.18 | all-reduce | flops 2048 | bytes 16384 | tf_op jit(solution)/shard_map/while/body/eval_jaxpr/psum | solution.py:138
  724.9 30.9 %all-reduce.16 = (f32[1024]{0:T(1024)S(1)}, f32[1024]{0:T(1024)S(1)}) all-reduce(f32[1024]{0:T(1024)S(1)} %get-tuple-element.2532, f32[1024]{0:T(1024)S(1)} %get-tuple-element.2533), channel_id=1, replica_groups=mesh['dp'=2,'segment'=4,'rows'=16] {'rows'}, use_global_device_ids=true, to_apply=%region_14.14 | all-reduce | flops 2048 | bytes 16384 | tf_op jit(solution)/shard_map/while/body/eval_jaxpr/psum | solution.py:138
  764.1 4.7 collective-permute-start.9
  777.0 29.9 %all-reduce.17 = (f32[1024]{0:T(1024)S(1)}, f32[1024]{0:T(1024)S(1)}) all-reduce(f32[1024]{0:T(1024)S(1)} %get-tuple-element.2554, f32[1024]{0:T(1024)S(1)} %get-tuple-element.2555), channel_id=1, replica_groups=mesh['dp'=2,'segment'=4,'rows'=16] {'rows'}, use_global_device_ids=true, to_apply=%region_18.18 | all-reduce | flops 2048 | bytes 16384 | tf_op jit(solution)/shard_map/while/body/eval_jaxpr/psum | solution.py:138
  839.0 30.9 %all-reduce.16 = (f32[1024]{0:T(1024)S(1)}, f32[1024]{0:T(1024)S(1)}) all-reduce(f32[1024]{0:T(1024)S(1)} %get-tuple-element.2532, f32[1024]{0:T(1024)S(1)} %get-tuple-element.2533), channel_id=1, replica_groups=mesh['dp'=2,'segment'=4,'rows'=16] {'rows'}, use_global_device_ids=true, to_apply=%region_14.14 | all-reduce | flops 2048 | bytes 16384 | tf_op jit(solution)/shard_map/while/body/eval_jaxpr/psum | solution.py:138
  891.0 29.9 %all-reduce.17 = (f32[1024]{0:T(1024)S(1)}, f32[1024]{0:T(1024)S(1)}) all-reduce(f32[1024]{0:T(1024)S(1)} %get-tuple-element.2554, f32[1024]{0:T(1024)S(1)} %get-tuple-element.2555), channel_id=1, replica_groups=mesh['dp'=2,'segment'=4,'rows'=16] {'rows'}, use_global_device_ids=true, to_apply=%region_18.18 | all-reduce | flops 2048 | bytes 16384 | tf_op jit(solution)/shard_map/while/body/eval_jaxpr/psum | solution.py:138
  956.3 31.2 %all-reduce.16 = (f32[1024]{0:T(1024)S(1)}, f32[1024]{0:T(1024)S(1)}) all-reduce(f32[1024]{0:T(1024)S(1)} %get-tuple-element.2532, f32[1024]{0:T(1024)S(1)} %get-tuple-element.2533), channel_id=1, replica_groups=mesh['dp'=2,'segment'=4,'rows'=16] {'rows'}, use_global_device_ids=true, to_apply=%region_14.14 | all-reduce | flops 2048 | bytes 16384 | tf_op jit(solution)/shard_map/while/body/eval_jaxpr/psum | solution.py:138
  1008.6 29.9 %all-reduce.17 = (f32[1024]{0:T(1024)S(1)}, f32[1024]{0:T(1024)S(1)}) all-reduce(f32[1024]{0:T(1024)S(1)} %get-tuple-element.2554, f32[1024]{0:T(1024)S(1)} %get-tuple-element.2555), channel_id=1, replica_groups=mesh['dp'=2,'segment'=4,'rows'=16] {'rows'}, use_global_device_ids=true, to_apply=%region_18.18 | all-reduce | flops 2048 | bytes 16384 | tf_op jit(solution)/shard_map/while/body/eval_jaxpr/psum | solution.py:138
  1071.5 31.2 %all-reduce.16 = (f32[1024]{0:T(1024)S(1)}, f32[1024]{0:T(1024)S(1)}) all-reduce(f32[1024]{0:T(1024)S(1)} %get-tuple-element.2532, f32[1024]{0:T(1024)S(1)} %get-tuple-element.2533), channel_id=1, replica_groups=mesh['dp'=2,'segment'=4,'rows'=16] {'rows'}, use_global_device_ids=true, to_apply=%region_14.14 | all-reduce | flops 2048 | bytes 16384 | tf_op jit(solution)/shard_map/while/body/eval_jaxpr/psum | solution.py:138
  1123.8 30.2 %all-reduce.17 = (f32[1024]{0:T(1024)S(1)}, f32[1024]{0:T(1024)S(1)}) all-reduce(f32[1024]{0:T(1024)S(1)} %get-tuple-element.2554, f32[1024]{0:T(1024)S(1)} %get-tuple-element.2555), channel_id=1, replica_groups=mesh['dp'=2,'segment'=4,'rows'=16] {'rows'}, use_global_device_ids=true, to_apply=%region_18.18 | all-reduce | flops 2048 | bytes 16384 | tf_op jit(solution)/shard_map/while/body/eval_jaxpr/psum | solution.py:138
  1164.7 292.2 %psum.135 = bf16[2,11,1024]{2,1,0:T(8,128)(2,1)S(1)} all-reduce(bf16[2,11,1024]{2,1,0:T(8,128)(2,1)S(1)} %convert_element_type.904), channel_id=1, replica_groups=mesh['dp'=2,'segment'=4,'rows'=16] {'dp','rows'}, use_global_device_ids=true, to_apply=%region_39.40 | all-reduce | flops 22528 | bytes 90112 | tf_op jit(solution)/shard_map/psum | solution.py:237
  (940 shorter events, 497.5 us)
Async XLA Ops:
  7.2 1451.0 %all-reduce.20.cloned.1.call-start = ((), (), s32[]{:S(2)}) async-start(), calls=%async_computation | async-start | bytes 8388608 | tf_op jit(solution)/shard_map/psum | solution.py:236
  19.3 11.5 collective-permute-start
  33.5 46.8 %collective-permute-start.1 = (bf16[2,2,32,1024]{3,2,1,0:T(8,128)(2,1)S(1)}, bf16[2,2,32,1024]{3,2,1,0:T(8,128)(2,1)}, u32[]{:S(2)}, u32[]{:S(2)}) collective-permute-start(bf16[2,2,32,1024]{3,2,1,0:T(8,128)(2,1)S(1)} %get-tuple-element.2433), channel_id=1, source_target_pairs={{1,0},{2,1},{3,2},{4,3},{5,4},{6,5},{7,6},{8,7},{9,8},{10,9},{11,1... | collective-permute-start | bytes 786440 | tf_op jit(solution)/shard_map/while/body/eval_jaxpr/ppermute | solution.py:24
  34.8 45.5 %collective-permute-start.2 = (bf16[2,2,32,1024]{3,2,1,0:T(8,128)(2,1)S(1)}, bf16[2,2,32,1024]{3,2,1,0:T(8,128)(2,1)}, u32[]{:S(2)}, u32[]{:S(2)}) collective-permute-start(bf16[2,2,32,1024]{3,2,1,0:T(8,128)(2,1)S(1)} %get-tuple-element.2433), channel_id=1, source_target_pairs={{0,1},{1,2},{2,3},{3,4},{4,5},{5,6},{6,7},{7,8},{8,9},{9,10},{10,1... | collective-permute-start | bytes 786440 | tf_op jit(solution)/shard_map/while/body/eval_jaxpr/ppermute | solution.py:22
  85.0 43.3 %collective-permute-start.3 = (bf16[2,2,32,1024]{3,2,1,0:T(8,128)(2,1)}, bf16[2,2,32,1024]{3,2,1,0:T(8,128)(2,1)}, u32[]{:S(2)}, u32[]{:S(2)}) collective-permute-start(bf16[2,2,32,1024]{3,2,1,0:T(8,128)(2,1)} %get-tuple-element.2454), channel_id=1, source_target_pairs={{1,0},{2,1},{3,2},{4,3},{5,4},{6,5},{7,6},{8,7},{9,8},{10,9},{11,1... | collective-permute-start | bytes 786440 | tf_op jit(solution)/shard_map/while/body/eval_jaxpr/ppermute | solution.py:24
  86.3 42.0 %collective-permute-start.4 = (bf16[2,2,32,1024]{3,2,1,0:T(8,128)(2,1)}, bf16[2,2,32,1024]{3,2,1,0:T(8,128)(2,1)}, u32[]{:S(2)}, u32[]{:S(2)}) collective-permute-start(bf16[2,2,32,1024]{3,2,1,0:T(8,128)(2,1)} %get-tuple-element.2454), channel_id=1, source_target_pairs={{0,1},{1,2},{2,3},{3,4},{4,5},{5,6},{6,7},{7,8},{8,9},{9,10},{10,1... | collective-permute-start | bytes 786440 | tf_op jit(solution)/shard_map/while/body/eval_jaxpr/ppermute | solution.py:22
  136.9 9.9 collective-permute-start
  149.4 42.6 %collective-permute-start.1 = (bf16[2,2,32,1024]{3,2,1,0:T(8,128)(2,1)S(1)}, bf16[2,2,32,1024]{3,2,1,0:T(8,128)(2,1)}, u32[]{:S(2)}, u32[]{:S(2)}) collective-permute-start(bf16[2,2,32,1024]{3,2,1,0:T(8,128)(2,1)S(1)} %get-tuple-element.2433), channel_id=1, source_target_pairs={{1,0},{2,1},{3,2},{4,3},{5,4},{6,5},{7,6},{8,7},{9,8},{10,9},{11,1... | collective-permute-start | bytes 786440 | tf_op jit(solution)/shard_map/while/body/eval_jaxpr/ppermute | solution.py:24
  150.7 41.3 %collective-permute-start.2 = (bf16[2,2,32,1024]{3,2,1,0:T(8,128)(2,1)S(1)}, bf16[2,2,32,1024]{3,2,1,0:T(8,128)(2,1)}, u32[]{:S(2)}, u32[]{:S(2)}) collective-permute-start(bf16[2,2,32,1024]{3,2,1,0:T(8,128)(2,1)S(1)} %get-tuple-element.2433), channel_id=1, source_target_pairs={{0,1},{1,2},{2,3},{3,4},{4,5},{5,6},{6,7},{7,8},{8,9},{9,10},{10,1... | collective-permute-start | bytes 786440 | tf_op jit(solution)/shard_map/while/body/eval_jaxpr/ppermute | solution.py:22
  196.7 43.3 %collective-permute-start.3 = (bf16[2,2,32,1024]{3,2,1,0:T(8,128)(2,1)}, bf16[2,2,32,1024]{3,2,1,0:T(8,128)(2,1)}, u32[]{:S(2)}, u32[]{:S(2)}) collective-permute-start(bf16[2,2,32,1024]{3,2,1,0:T(8,128)(2,1)} %get-tuple-element.2454), channel_id=1, source_target_pairs={{1,0},{2,1},{3,2},{4,3},{5,4},{6,5},{7,6},{8,7},{9,8},{10,9},{11,1... | collective-permute-start | bytes 786440 | tf_op jit(solution)/shard_map/while/body/eval_jaxpr/ppermute | solution.py:24
  198.0 42.0 %collective-permute-start.4 = (bf16[2,2,32,1024]{3,2,1,0:T(8,128)(2,1)}, bf16[2,2,32,1024]{3,2,1,0:T(8,128)(2,1)}, u32[]{:S(2)}, u32[]{:S(2)}) collective-permute-start(bf16[2,2,32,1024]{3,2,1,0:T(8,128)(2,1)} %get-tuple-element.2454), channel_id=1, source_target_pairs={{0,1},{1,2},{2,3},{3,4},{4,5},{5,6},{6,7},{7,8},{8,9},{9,10},{10,1... | collective-permute-start | bytes 786440 | tf_op jit(solution)/shard_map/while/body/eval_jaxpr/ppermute | solution.py:22
  248.6 10.5 collective-permute-start
  261.8 42.6 %collective-permute-start.1 = (bf16[2,2,32,1024]{3,2,1,0:T(8,128)(2,1)S(1)}, bf16[2,2,32,1024]{3,2,1,0:T(8,128)(2,1)}, u32[]{:S(2)}, u32[]{:S(2)}) collective-permute-start(bf16[2,2,32,1024]{3,2,1,0:T(8,128)(2,1)S(1)} %get-tuple-element.2433), channel_id=1, source_target_pairs={{1,0},{2,1},{3,2},{4,3},{5,4},{6,5},{7,6},{8,7},{9,8},{10,9},{11,1... | collective-permute-start | bytes 786440 | tf_op jit(solution)/shard_map/while/body/eval_jaxpr/ppermute | solution.py:24
  263.1 41.3 %collective-permute-start.2 = (bf16[2,2,32,1024]{3,2,1,0:T(8,128)(2,1)S(1)}, bf16[2,2,32,1024]{3,2,1,0:T(8,128)(2,1)}, u32[]{:S(2)}, u32[]{:S(2)}) collective-permute-start(bf16[2,2,32,1024]{3,2,1,0:T(8,128)(2,1)S(1)} %get-tuple-element.2433), channel_id=1, source_target_pairs={{0,1},{1,2},{2,3},{3,4},{4,5},{5,6},{6,7},{7,8},{8,9},{9,10},{10,1... | collective-permute-start | bytes 786440 | tf_op jit(solution)/shard_map/while/body/eval_jaxpr/ppermute | solution.py:22
  309.1 42.7 %collective-permute-start.3 = (bf16[2,2,32,1024]{3,2,1,0:T(8,128)(2,1)}, bf16[2,2,32,1024]{3,2,1,0:T(8,128)(2,1)}, u32[]{:S(2)}, u32[]{:S(2)}) collective-permute-start(bf16[2,2,32,1024]{3,2,1,0:T(8,128)(2,1)} %get-tuple-element.2454), channel_id=1, source_target_pairs={{1,0},{2,1},{3,2},{4,3},{5,4},{6,5},{7,6},{8,7},{9,8},{10,9},{11,1... | collective-permute-start | bytes 786440 | tf_op jit(solution)/shard_map/while/body/eval_jaxpr/ppermute | solution.py:24
  310.4 41.5 %collective-permute-start.4 = (bf16[2,2,32,1024]{3,2,1,0:T(8,128)(2,1)}, bf16[2,2,32,1024]{3,2,1,0:T(8,128)(2,1)}, u32[]{:S(2)}, u32[]{:S(2)}) collective-permute-start(bf16[2,2,32,1024]{3,2,1,0:T(8,128)(2,1)} %get-tuple-element.2454), channel_id=1, source_target_pairs={{0,1},{1,2},{2,3},{3,4},{4,5},{5,6},{6,7},{7,8},{8,9},{9,10},{10,1... | collective-permute-start | bytes 786440 | tf_op jit(solution)/shard_map/while/body/eval_jaxpr/ppermute | solution.py:22
  360.4 10.1 collective-permute-start
  373.1 42.6 %collective-permute-start.1 = (bf16[2,2,32,1024]{3,2,1,0:T(8,128)(2,1)S(1)}, bf16[2,2,32,1024]{3,2,1,0:T(8,128)(2,1)}, u32[]{:S(2)}, u32[]{:S(2)}) collective-permute-start(bf16[2,2,32,1024]{3,2,1,0:T(8,128)(2,1)S(1)} %get-tuple-element.2433), channel_id=1, source_target_pairs={{1,0},{2,1},{3,2},{4,3},{5,4},{6,5},{7,6},{8,7},{9,8},{10,9},{11,1... | collective-permute-start | bytes 786440 | tf_op jit(solution)/shard_map/while/body/eval_jaxpr/ppermute | solution.py:24
  374.4 41.3 %collective-permute-start.2 = (bf16[2,2,32,1024]{3,2,1,0:T(8,128)(2,1)S(1)}, bf16[2,2,32,1024]{3,2,1,0:T(8,128)(2,1)}, u32[]{:S(2)}, u32[]{:S(2)}) collective-permute-start(bf16[2,2,32,1024]{3,2,1,0:T(8,128)(2,1)S(1)} %get-tuple-element.2433), channel_id=1, source_target_pairs={{0,1},{1,2},{2,3},{3,4},{4,5},{5,6},{6,7},{7,8},{8,9},{9,10},{10,1... | collective-permute-start | bytes 786440 | tf_op jit(solution)/shard_map/while/body/eval_jaxpr/ppermute | solution.py:22
  420.5 42.4 %collective-permute-start.3 = (bf16[2,2,32,1024]{3,2,1,0:T(8,128)(2,1)}, bf16[2,2,32,1024]{3,2,1,0:T(8,128)(2,1)}, u32[]{:S(2)}, u32[]{:S(2)}) collective-permute-start(bf16[2,2,32,1024]{3,2,1,0:T(8,128)(2,1)} %get-tuple-element.2454), channel_id=1, source_target_pairs={{1,0},{2,1},{3,2},{4,3},{5,4},{6,5},{7,6},{8,7},{9,8},{10,9},{11,1... | collective-permute-start | bytes 786440 | tf_op jit(solution)/shard_map/while/body/eval_jaxpr/ppermute | solution.py:24
  421.8 41.1 %collective-permute-start.4 = (bf16[2,2,32,1024]{3,2,1,0:T(8,128)(2,1)}, bf16[2,2,32,1024]{3,2,1,0:T(8,128)(2,1)}, u32[]{:S(2)}, u32[]{:S(2)}) collective-permute-start(bf16[2,2,32,1024]{3,2,1,0:T(8,128)(2,1)} %get-tuple-element.2454), channel_id=1, source_target_pairs={{0,1},{1,2},{2,3},{3,4},{4,5},{5,6},{6,7},{7,8},{8,9},{9,10},{10,1... | collective-permute-start | bytes 786440 | tf_op jit(solution)/shard_map/while/body/eval_jaxpr/ppermute | solution.py:22
  471.4 9.8 collective-permute-start
  483.8 42.8 %collective-permute-start.1 = (bf16[2,2,32,1024]{3,2,1,0:T(8,128)(2,1)S(1)}, bf16[2,2,32,1024]{3,2,1,0:T(8,128)(2,1)}, u32[]{:S(2)}, u32[]{:S(2)}) collective-permute-start(bf16[2,2,32,1024]{3,2,1,0:T(8,128)(2,1)S(1)} %get-tuple-element.2433), channel_id=1, source_target_pairs={{1,0},{2,1},{3,2},{4,3},{5,4},{6,5},{7,6},{8,7},{9,8},{10,9},{11,1... | collective-permute-start | bytes 786440 | tf_op jit(solution)/shard_map/while/body/eval_jaxpr/ppermute | solution.py:24
  485.1 41.5 %collective-permute-start.2 = (bf16[2,2,32,1024]{3,2,1,0:T(8,128)(2,1)S(1)}, bf16[2,2,32,1024]{3,2,1,0:T(8,128)(2,1)}, u32[]{:S(2)}, u32[]{:S(2)}) collective-permute-start(bf16[2,2,32,1024]{3,2,1,0:T(8,128)(2,1)S(1)} %get-tuple-element.2433), channel_id=1, source_target_pairs={{0,1},{1,2},{2,3},{3,4},{4,5},{5,6},{6,7},{7,8},{8,9},{9,10},{10,1... | collective-permute-start | bytes 786440 | tf_op jit(solution)/shard_map/while/body/eval_jaxpr/ppermute | solution.py:22
  531.3 42.5 %collective-permute-start.3 = (bf16[2,2,32,1024]{3,2,1,0:T(8,128)(2,1)}, bf16[2,2,32,1024]{3,2,1,0:T(8,128)(2,1)}, u32[]{:S(2)}, u32[]{:S(2)}) collective-permute-start(bf16[2,2,32,1024]{3,2,1,0:T(8,128)(2,1)} %get-tuple-element.2454), channel_id=1, source_target_pairs={{1,0},{2,1},{3,2},{4,3},{5,4},{6,5},{7,6},{8,7},{9,8},{10,9},{11,1... | collective-permute-start | bytes 786440 | tf_op jit(solution)/shard_map/while/body/eval_jaxpr/ppermute | solution.py:24
  532.6 41.3 %collective-permute-start.4 = (bf16[2,2,32,1024]{3,2,1,0:T(8,128)(2,1)}, bf16[2,2,32,1024]{3,2,1,0:T(8,128)(2,1)}, u32[]{:S(2)}, u32[]{:S(2)}) collective-permute-start(bf16[2,2,32,1024]{3,2,1,0:T(8,128)(2,1)} %get-tuple-element.2454), channel_id=1, source_target_pairs={{0,1},{1,2},{2,3},{3,4},{4,5},{5,6},{6,7},{7,8},{8,9},{9,10},{10,1... | collective-permute-start | bytes 786440 | tf_op jit(solution)/shard_map/while/body/eval_jaxpr/ppermute | solution.py:22
  648.5 9.7 collective-permute-start.8
  762.8 9.7 collective-permute-start.8
  876.9 9.7 collective-permute-start.8
  927.2 9.8 collective-permute-start.5
  994.5 9.7 collective-permute-start.8
  1109.7 9.7 collective-permute-start.8
  (285 other events, 2854.3 us)
Sparse Core Ops, SparseCore 0:
  1164.0 275.1 all-reduce.19
where the time goes:
time: 1470 us
  blocking collectives  902 us (61%)
  other arithmetic  184 us (13%)
  local copies, waits for them, and re-layouts  142 us (10%)
  starting transfers between devices  137 us (9%)
  matrix products  67 us (5%)
  between operations  20.1 us (1%)
    psum x10, blocking collectives, backward_cell(): total_a, total_b = lax.psum((part_a, part_b), 'rows')  306 us
    psum x10, blocking collectives, forward_cell(): lax.psum((jnp.sum(wide_input, axis=(0, 1, 2)), jnp.sum(wide_input * wide_...  304 us
    psum x1, blocking collectives, local(): lax.psum(small_part.astype(jnp.bfloat16), ('dp', 'rows'))  292 us
    ppermute x20, starting transfers between devices, padded_2(): lax.ppermute(tail, axis, [(i, (i + 1) % count) for i in range(ends)])  90.6 us
    dynamic_update_slice x40, other arithmetic, put_at(): return lax.dynamic_update_slice(store, fresh, anchor)  70.7 us
    dynamic_slice x50, local copies, waits for them, and re-layouts, put_at(): previous = lax.dynamic_slice(store, anchor, extent).reshape(current.shape)  64.1 us
    dot_general x10, matrix products, backward_cell(): lax.dot_general(gradient.reshape(-1, channels), pointwise[cell_slot], (((...  46.1 us
  transfers between devices with their start and end apart: 51, of which 6 were waited for; matrix products, arithmetic and copies ran while one was open for 11% of the time, Pallas kernels for 0%

commit v1 on v0

v1 whole, which is shorter than its diff:
```python
import functools

import jax
import jax.numpy as jnp
from jax import lax
from jax.experimental import pallas as pl
from jax.experimental.pallas import tpu as pltpu
from jax.sharding import PartitionSpec as P

DMAX = 2
MICRO = 2
IMG = 2
EPSILON = 1e-05
MESH = pl.DeviceIdType.MESH
LANES = 128
SUB = 8
F32 = jnp.float32
BF16 = jnp.bfloat16


def window_kernel(
    geo,
    x_ref,
    cot_ref,
    w_hbm,
    par_ref,
    act_ref,
    dil_ref,
    sec_out,
    hid_out,
    grad_out,
    small_out,
    wv,
    xs,
    xpos,
    apos,
    hpos,
    ghpos,
    gppos,
    gpos,
    gnat,
    hs,
    gs,
    gpn,
    gph,
    coth,
    stat_own,
    stat_in,
    norms,
    small,
    sec_in,
    hid_in,
    grad_in,
    small_in,
    w_sem,
    stat_ss,
    stat_rs,
    halo_ss,
    halo_rs,
    own_ss,
    own_rs,
    copy_sem,
):
    slots, segs, row_devs, local_rows, cols, chans = geo
    per = slots // segs
    half = segs // MICRO
    group = half * row_devs
    pos = local_rows * cols
    groups = chans // LANES
    wide = cols + 2 * DMAX
    chunks = cols // SUB
    population = IMG * local_rows * row_devs * cols
    seg = lax.axis_index("segment")
    row = lax.axis_index("rows")
    micro = seg // half
    gid = (seg % half) * row_devs + row
    up = (row + row_devs - 1) % row_devs
    down = (row + 1) % row_devs
    has_up = row > 0
    has_down = row < row_devs - 1

    def peer(k):
        other = (gid + k) % group
        return {"segment": micro * half + other // row_devs, "rows": other % row_devs}

    def greet(k, carry):
        pl.semaphore_signal(barrier, inc=1, device_id=peer(k), device_id_type=MESH)
        return carry

    for j in range(slots):
        pltpu.make_async_copy(w_hbm.at[j], wv.at[j], w_sem.at[j]).start()

    barrier = pltpu.get_barrier_semaphore()
    lax.fori_loop(1, group, greet, 0)
    outside = segs - half
    for k in range(outside):
        other = (micro * half + half + k) % segs
        pl.semaphore_signal(barrier, inc=1, device_id={"segment": other}, device_id_type=MESH)
    pl.semaphore_wait(barrier, group - 1 + outside)

    def halo_sends(step, src, up_dst, down_dst):
        a = pltpu.make_async_remote_copy(
            src, up_dst, halo_ss.at[step, 0], halo_rs.at[step, 0],
            device_id={"rows": up}, device_id_type=MESH)
        b = pltpu.make_async_remote_copy(
            src, down_dst, halo_ss.at[step, 1], halo_rs.at[step, 1],
            device_id={"rows": down}, device_id_type=MESH)
        return a, b

    def cot_sends():
        return halo_sends(2 * slots, cot_ref, coth.at[1], coth.at[0])

    def fwd_sends(j):
        return halo_sends(j, xs.at[j, 1], xs.at[j, 2], xs.at[j, 0])

    def bwd_sends(j):
        return halo_sends(slots + j, gpn.at[j], gph.at[j, 1], gph.at[j, 0])

    def stat_send(step, k):
        return pltpu.make_async_remote_copy(
            stat_own.at[step], stat_in.at[step, k - 1], stat_ss.at[step], stat_rs.at[step],
            device_id=peer(k), device_id_type=MESH)

    def push_stats(step):
        def body(k, carry):
            stat_send(step, k).start()
            return carry
        lax.fori_loop(1, group, body, 0)

    def stats_whole(step):
        return pltpu.make_async_remote_copy(
            stat_in.at[step], stat_in.at[step], stat_ss.at[step], stat_rs.at[step],
            device_id=peer(1), device_id_type=MESH)

    def to_owner(src, dst, slot, kind, owner):
        return pltpu.make_async_remote_copy(
            src, dst, own_ss.at[slot, kind], own_rs.at[slot % per, kind],
            device_id={"segment": owner}, device_id_type=MESH)

    def give(src, dst, slot, kind, owner):
        @pl.when(seg != owner)
        def _():
            to_owner(src, dst, slot, kind, owner).start()

        @pl.when(seg == owner)
        def _():
            pltpu.make_async_copy(src, dst, copy_sem.at[slot, kind]).start()

    def given(src, dst, slot, kind, owner):
        @pl.when(seg != owner)
        def _():
            to_owner(src, dst, slot, kind, owner).wait_send()

        @pl.when(seg == owner)
        def _():
            pltpu.make_async_copy(src, dst, copy_sem.at[slot, kind]).wait()

    def hid_args(j):
        return hs.at[j], hid_in.at[j % per, (seg - j // per + segs) % segs], j, 0, j // per

    def grad_args(j):
        return gs.at[j], grad_in.at[j % per, (seg - j // per + segs) % segs], j, 1, j // per

    def small_args(j):
        return small.at[j], small_in.at[j % per, (seg - j // per + segs) % segs], j, 2, j // per

    def sec_args(j):
        return xs.at[j + 1, 1], sec_in.at[seg], j, 3, j // per

    for a in cot_sends():
        a.start()

    xs[0, 1] = x_ref[...]

    edge = jnp.zeros((DMAX * SUB, LANES), F32)

    def clear(j, carry):
        for r in range(3 * local_rows):
            apos[j, pl.ds(r * wide * SUB, DMAX * SUB), :] = edge
            apos[j, pl.ds((r * wide + DMAX + cols) * SUB, DMAX * SUB), :] = edge
        return carry

    lax.fori_loop(0, slots, clear, 0)
    for r in range(3 * local_rows):
        ghpos[pl.ds(r * wide * SUB, DMAX * SUB), :] = edge
        ghpos[pl.ds((r * wide + DMAX + cols) * SUB, DMAX * SUB), :] = edge

    def param(j, t):
        return par_ref[j, pl.ds(t * SUB, SUB), :]

    def tiles(value):
        return value.reshape(value.shape[0] // SUB, SUB, LANES)

    def flat(value):
        return value.reshape(-1, LANES)

    def spread_out(src, dst, base):
        for g in range(groups):
            dst[pl.ds(base * SUB + g, pos, stride=SUB), :] = src[:, g * LANES : (g + 1) * LANES].astype(F32)

    def own_rows(chunk):
        return chunk // chunks, chunk % chunks

    def at(p):
        return pl.ds(pl.multiple_of(p * SUB, SUB), SUB * SUB)

    def row_ok(value, r):
        if r < local_rows:
            return jnp.where(has_up, value, 0.0)
        if r >= 2 * local_rows:
            return jnp.where(has_down, value, 0.0)
        return value

    zero = jnp.zeros((SUB, LANES), F32)

    def reach(ref, lead, r, c, two):
        found = []
        for a in (-1, 0, 1):
            for b in (-1, 0, 1):
                both = [
                    tiles(ref[lead + (at((r + a * d) * wide + DMAX + c * SUB + b * d), slice(None))])
                    for d in ((1, 2) if a or b else (1,))
                ]
                found.append(jnp.where(two, both[1], both[0]) if len(both) > 1 else both[0])
        return found

    def switch(ref, j, shape):
        return jnp.full(shape, ref[j], F32) > 0.5

    def forward(j, carry):
        spread_out(xs.at[j, 1], xpos.at[j], pos)

        def sums(chunk, acc):
            v = tiles(xpos[j, at(pos + chunk * SUB), :])
            return acc[0] + jnp.sum(v, axis=0), acc[1] + jnp.sum(v * v, axis=0)

        s1, s2 = lax.fori_loop(0, pos // SUB, sums, (zero, zero))
        stat_own[j, 0:SUB, :] = s1
        stat_own[j, SUB : 2 * SUB, :] = s2
        push_stats(j)
        for a in fwd_sends(j):
            a.start()
        stats_whole(j).wait_recv()
        total = jnp.sum(stat_in[j], axis=0) + stat_own[j]
        center = total[0:SUB] / population
        spread = total[SUB : 2 * SUB] / population - center * center
        scaling = lax.rsqrt(spread + EPSILON)
        norms[j, 0:SUB, :] = center
        norms[j, SUB : 2 * SUB, :] = scaling
        gain = param(j, 9)
        shift = param(j, 10)

        def activate(r):
            def body(chunk, carry):
                v = tiles(xpos[j, at(r * cols + chunk * SUB), :])
                v = jnp.maximum((v - center) * scaling * gain + shift, 0.0)
                v = row_ok(v, r).astype(BF16).astype(F32)
                apos[j, at(r * wide + DMAX + chunk * SUB), :] = flat(v)
                return carry
            lax.fori_loop(0, chunks, body, 0)

        for r in range(local_rows, 2 * local_rows):
            activate(r)
        for side in range(2):
            fwd_sends(j)[side].wait_recv()
        spread_out(xs.at[j, 0], xpos.at[j], 0)
        spread_out(xs.at[j, 2], xpos.at[j], 2 * pos)
        for r in range(local_rows):
            activate(r)
            activate(2 * local_rows + r)
        two = switch(dil_ref, j, (SUB, SUB, LANES))
        taps = [param(j, t) for t in range(9)]

        def mix(chunk, carry):
            r, c = own_rows(chunk)
            acc = jnp.zeros((SUB, SUB, LANES), F32)
            for v, tap in zip(reach(apos, (j,), local_rows + r, c, two), taps):
                acc = acc + v * tap
            hpos[at(chunk * SUB), :] = flat(acc)
            return carry

        lax.fori_loop(0, pos // SUB, mix, 0)
        for g in range(groups):
            hs[j, :, g * LANES : (g + 1) * LANES] = hpos[pl.ds(g, pos, stride=SUB), :].astype(BF16)
        give(*hid_args(j))
        pltpu.make_async_copy(w_hbm.at[j], wv.at[j], w_sem.at[j]).wait()
        step = chans // 4
        active = switch(act_ref, j, (pos, step))
        for n in range(4):
            cut = slice(n * step, (n + 1) * step)
            mixed = jnp.dot(hs[j], wv[j, :, cut], preferred_element_type=F32)
            old = xs[j, 1, :, cut].astype(F32)
            xs[j + 1, 1, :, cut] = jnp.where(active, old + mixed, old).astype(BF16)

        @pl.when(j % per == per - 1)
        def _():
            give(*sec_args(j))

        return carry

    lax.fori_loop(0, slots, forward, 0)

    for a in cot_sends():
        a.wait_recv()
    for side, src in enumerate((coth.at[0], cot_ref, coth.at[1])):
        for g in range(groups):
            v = src[:, g * LANES : (g + 1) * LANES].astype(F32)
            v = row_ok(v, side * local_rows)
            gpos[pl.ds(side * pos * SUB + g, pos, stride=SUB), :] = v
            gnat[side * pos : (side + 1) * pos, g * LANES : (g + 1) * LANES] = v.astype(BF16)

    def backward(t, carry):
        j = slots - 1 - t
        step = slots + j
        active = switch(act_ref, j, (SUB, SUB, LANES))
        live = switch(act_ref, j, (SUB, LANES))
        gs[j] = jnp.where(
            switch(act_ref, j, (pos, chans)), gnat[pos : 2 * pos, :].astype(F32), 0.0).astype(BF16)
        give(*grad_args(j))
        width = chans // 4
        for n in range(4):
            gh = lax.dot_general(
                gnat[...], wv[j, n * width : (n + 1) * width, :],
                (((1,), (1,)), ((), ())), preferred_element_type=F32)
            gh = gh.astype(BF16).astype(F32)
            for k in range(width // LANES):
                g = n * (width // LANES) + k
                for r in range(3 * local_rows):
                    ghpos[pl.ds((r * wide + DMAX) * SUB + g, cols, stride=SUB), :] = gh[
                        r * cols : (r + 1) * cols, k * LANES : (k + 1) * LANES]
        two = switch(dil_ref, j, (SUB, SUB, LANES))
        taps = [param(j, k) for k in range(9)]
        gain = param(j, 9)
        shift = param(j, 10)
        center = norms[j, 0:SUB, :]
        scaling = norms[j, SUB : 2 * SUB, :]

        def pull(chunk, acc):
            r, c = own_rows(chunk)
            total = jnp.zeros((SUB, SUB, LANES), F32)
            for v, tap in zip(reach(ghpos, (), local_rows + r, c, two), taps[::-1]):
                total = total + v * tap
            normed = (tiles(xpos[j, at(pos + chunk * SUB), :]) - center) * scaling
            total = jnp.where(normed * gain + shift > 0, total, 0.0)
            gppos[at(pos + chunk * SUB), :] = flat(total)
            return acc[0] + jnp.sum(total, axis=0), acc[1] + jnp.sum(total * normed, axis=0)

        sum_a, sum_b = lax.fori_loop(0, pos // SUB, pull, (zero, zero))
        stat_own[step, 0:SUB, :] = sum_a
        stat_own[step, SUB : 2 * SUB, :] = sum_b

        @pl.when(j > 0)
        def _():
            push_stats(step)
            for g in range(groups):
                gpn[j, :, g * LANES : (g + 1) * LANES] = gppos[
                    pl.ds(pos * SUB + g, pos, stride=SUB), :].astype(BF16)
            for a in bwd_sends(j):
                a.start()

        def tap_grads(chunk, acc):
            r, c = own_rows(chunk)
            gh = tiles(ghpos[at((local_rows + r) * wide + DMAX + c * SUB), :])
            found = reach(apos, (j,), local_rows + r, c, two)
            return tuple(t + jnp.sum(v * gh, axis=0) for t, v in zip(acc, found))

        terms = lax.fori_loop(0, pos // SUB, tap_grads, (zero,) * 9)
        for k, term in enumerate(terms + (sum_b, sum_a)):
            small[j, k * SUB : (k + 1) * SUB, :] = jnp.where(live, term, 0.0)
        give(*small_args(j))

        @pl.when(j > 0)
        def _():
            stats_whole(step).wait_recv()
            total = jnp.sum(stat_in[step], axis=0) + stat_own[step]
            mean_a = total[0:SUB] / population
            mean_b = total[SUB : 2 * SUB] / population
            for side in range(2):
                bwd_sends(j)[side].wait_recv()
            spread_out(gph.at[j, 0], gppos, 0)
            spread_out(gph.at[j, 1], gppos, 2 * pos)
            factor = scaling * gain
            for r in range(3 * local_rows):
                def body(chunk, carry):
                    where = at(r * cols + chunk * SUB)
                    normed = (tiles(xpos[j, where, :]) - center) * scaling
                    old = tiles(gpos[where, :])
                    new = old + factor * (tiles(gppos[where, :]) - mean_a - normed * mean_b)
                    new = row_ok(jnp.where(active, new, old), r).astype(BF16).astype(F32)
                    gpos[where, :] = flat(new)
                    return carry
                lax.fori_loop(0, chunks, body, 0)
            for g in range(groups):
                gnat[:, g * LANES : (g + 1) * LANES] = gpos[pl.ds(g, 3 * pos, stride=SUB), :].astype(BF16)

        return carry

    lax.fori_loop(0, slots, backward, 0)

    def finish(j, carry):
        given(*hid_args(j))
        given(*grad_args(j))
        given(*small_args(j))
        for a in fwd_sends(j):
            a.wait_send()
        stats_whole(j).wait_send()

        @pl.when(j % per == per - 1)
        def _():
            given(*sec_args(j))

        @pl.when(j > 0)
        def _():
            for a in bwd_sends(j):
                a.wait_send()
            stats_whole(slots + j).wait_send()

        return carry

    lax.fori_loop(0, slots, finish, 0)
    for a in cot_sends():
        a.wait_send()

    def landed(dst, slot, kind):
        to_owner(dst, dst, slot, kind, (seg + 1) % segs).wait_recv()

    for k in range(per):
        landed(hid_in.at[k, pl.ds(1, segs - 1)], k, 0)
        landed(grad_in.at[k, pl.ds(1, segs - 1)], k, 1)
        landed(small_in.at[k, pl.ds(1, segs - 1)], k, 2)
    landed(sec_in.at[pl.ds(1, segs - 1)], per - 1, 3)
    sec_out[...] = sec_in[...]
    hid_out[...] = hid_in[...]
    grad_out[...] = grad_in[...]
    small_out[...] = jnp.sum(small_in[...], axis=1)


def run_window(geo, x, cot, weights, params, active, dilations):
    slots, segs, row_devs, local_rows, cols, chans = geo
    per = slots // segs
    pos = local_rows * cols
    group = segs // MICRO * row_devs
    wide = cols + 2 * DMAX
    ext = 3 * local_rows * wide * SUB
    vm = pltpu.VMEM
    dma = pltpu.SemaphoreType.DMA
    vmem = pl.BlockSpec(memory_space=pltpu.VMEM)
    smem = pl.BlockSpec(memory_space=pltpu.SMEM)
    return pl.pallas_call(
        functools.partial(window_kernel, geo),
        out_shape=(
            jax.ShapeDtypeStruct((segs, pos, chans), BF16),
            jax.ShapeDtypeStruct((per, segs, pos, chans), BF16),
            jax.ShapeDtypeStruct((per, segs, pos, chans), BF16),
            jax.ShapeDtypeStruct((per, 11 * SUB, LANES), F32),
        ),
        in_specs=[vmem, vmem, pl.BlockSpec(memory_space=pl.ANY), vmem, smem, smem],
        out_specs=(vmem,) * 4,
        scratch_shapes=[
            vm((slots, chans, chans), BF16),
            vm((slots + 1, 3, pos, chans), BF16),
            vm((slots, 3 * pos * SUB, LANES), F32),
            vm((slots, ext, LANES), F32),
            vm((pos * SUB, LANES), F32),
            vm((ext, LANES), F32),
            vm((3 * pos * SUB, LANES), F32),
            vm((3 * pos * SUB, LANES), F32),
            vm((3 * pos, chans), BF16),
            vm((slots, pos, chans), BF16),
            vm((slots, pos, chans), BF16),
            vm((slots, pos, chans), BF16),
            vm((slots, 2, pos, chans), BF16),
            vm((2, pos, chans), BF16),
            vm((2 * slots, 2 * SUB, LANES), F32),
            vm((2 * slots, group - 1, 2 * SUB, LANES), F32),
            vm((slots, 2 * SUB, LANES), F32),
            vm((slots, 11 * SUB, LANES), F32),
            vm((segs, pos, chans), BF16),
            vm((per, segs, pos, chans), BF16),
            vm((per, segs, pos, chans), BF16),
            vm((per, segs, 11 * SUB, LANES), F32),
            dma((slots,)),
            dma((2 * slots,)),
            dma((2 * slots,)),
            dma((2 * slots + 1, 2)),
            dma((2 * slots + 1, 2)),
            dma((slots, 4)),
            dma((per, 4)),
            dma((slots, 4)),
        ],
        compiler_params=pltpu.CompilerParams(
            collective_id=0, has_side_effects=True, vmem_limit_bytes=64000 * 1024),
        name="window",
    )(x, cot, weights, params, active, dilations)


def local(images, cotangent, pointwise, depthwise, norm_gain, norm_shift, cell_counts, dilations):
    segs = lax.axis_size("segment")
    row_devs = lax.axis_size("rows")
    dps = lax.axis_size("dp")
    seg = lax.axis_index("segment")
    per, chans = pointwise.shape[0], pointwise.shape[2]
    count, local_rows, cols, _ = images.shape
    slots = per * segs
    pos = local_rows * cols
    geo = (slots, segs, row_devs, local_rows, cols, chans)
    x = lax.dynamic_index_in_dim(images.reshape(count, pos, chans), seg, 0, keepdims=False)
    cot = lax.dynamic_index_in_dim(cotangent.reshape(count, pos, chans), seg, 0, keepdims=False)
    part = chans // dps
    mine = lax.dynamic_slice_in_dim(pointwise, lax.axis_index("dp") * part, part, 1)
    weights = lax.all_gather(mine, "segment", axis=0, tiled=True)
    weights = lax.all_gather(weights, "dp", axis=1, tiled=True)
    flags = (jnp.arange(per, dtype=jnp.int32) < cell_counts[0]).astype(F32)
    pack = jnp.concatenate(
        [depthwise, norm_gain[:, None], norm_shift[:, None],
         jnp.broadcast_to(flags[:, None, None], (per, 1, chans)),
         jnp.broadcast_to((dilations > 1).astype(F32)[:, None, None], (per, 1, chans))], axis=1)
    pack = lax.all_gather(pack, "segment", axis=0, tiled=True)
    active = pack[:, 11, 0]
    rates = pack[:, 12, 0]
    params = pack[:, :11].reshape(slots, 11 * SUB, LANES)
    sec, hid, grad, small = run_window(geo, x, cot, weights, params, active, rates)
    hid = hid.reshape(per, segs * pos, chans)
    grad = grad.reshape(per, segs * pos, chans)
    part_w = lax.dot_general(hid, grad, (((1,), (1,)), ((0,), (0,))), preferred_element_type=F32)
    small = jnp.swapaxes(small.reshape(per, 11, chans), 1, 2)
    small = jnp.pad(small, ((0, 0), (0, 0), (0, LANES - 11)))
    both = jnp.concatenate([part_w.astype(BF16), small.astype(BF16)], axis=2)
    both = lax.psum_scatter(both, ("dp", "rows"), scatter_dimension=1, tiled=True).astype(F32)
    grad_small = jnp.swapaxes(both[:, :, chans : chans + 11], 1, 2)
    return (
        sec.reshape(1, count, local_rows, cols, chans),
        both[:, :, :chans],
        grad_small[:, :9],
        grad_small[:, 9:],
    )


def solution(mesh):
    return jax.shard_map(
        local,
        mesh=mesh,
        in_specs=(
            P("dp", "rows", None, None),
            P("dp", "rows", None, None),
            P("segment", None, None),
            P("segment", None, None),
            P("segment", None),
            P("segment", None),
            P("segment"),
            P("segment"),
        ),
        out_specs=(
            P("segment", "dp", "rows", None, None),
            P("segment", ("dp", "rows"), None),
            P("segment", None, ("dp", "rows")),
            P("segment", None, ("dp", "rows")),
        ),
        check_vma=False,
    )
```

time: 1470 us -> 447 us (0.30)
  blocking collectives: 902 us -> 10.2 us
  waiting for transfers between devices: 9.84 us -> 225 us
  other arithmetic: 184 us -> 4.32 us
  Pallas kernels: 0 us -> 164 us
  starting transfers between devices: 137 us -> 0.12 us
  local copies, waits for them, and re-layouts: 142 us -> 23.5 us
  matrix products: 67 us -> 2.84 us
    psum x21 -> x0, blocking collectives: 902 us -> none  [the longest x10 306 us: backward_cell(): total_a, total_b = lax.psum((part_a, part_b), 'rows')]
    pallas_call x0 -> x1, Pallas kernels: none -> 164 us  [run_window(): pl.pallas_call(functools.partial(window_kernel, geo), out_shape=(jax.Shap...]
    ppermute x50 -> x0, starting transfers between devices: 137 us -> none  [the longest x20 90.6 us: padded_2(): lax.ppermute(tail, axis, [(i, (i + 1) % count) for i in range(ends)])]
    unnamed x1 -> x4, waiting for transfers between devices: 0.02 us -> 118 us
    all_gather x0 -> x2, waiting for transfers between devices: none -> 108 us  [the longest x1 86.1 us: local(): weights = lax.all_gather(mine, 'segment', axis=0, tiled=True)]
    dynamic_slice x85 -> x1, local copies, waits for them, and re-layouts: 77.3 us -> 3.11 us  [local(): lax.dynamic_slice_in_dim(pointwise, lax.axis_index('dp') * part, part, 1)]
    dynamic_update_slice x40 -> x0, other arithmetic: 70.7 us -> none  [put_at(): return lax.dynamic_update_slice(store, fresh, anchor)]
    dot_general x22 -> x1, matrix products: 67 us -> 2.84 us  [local(): lax.dot_general(hid, grad, (((1,), (1,)), ((0,), (0,))), preferred_elemen...]
  transfers between devices with their start and end apart: 51 -> 3, of which waited for: 6 -> 3; matrix products, arithmetic and copies ran while one was open for 11% -> 1% of each run, Pallas kernels for 0% -> 0%
where the time goes in v1:
time: 447 us; the launch traced here: 446 us
  waiting for transfers between devices  225 us (50%)
  Pallas kernels  164 us (37%)
  local copies, waits for them, and re-layouts  23.5 us (5%)
  between operations  15.2 us (3%)
  blocking collectives  10.2 us (2%)
    pallas_call x1, Pallas kernels, run_window(): pl.pallas_call(functools.partial(window_kernel, geo), out_shape=(jax.Shap...  164 us
    unnamed x4, waiting for transfers between devices  118 us
    all_gather x1, waiting for transfers between devices, local(): weights = lax.all_gather(mine, 'segment', axis=0, tiled=True)  86.1 us
    all_gather x1, waiting for transfers between devices, local(): weights = lax.all_gather(weights, 'dp', axis=1, tiled=True)  21.5 us
    concatenate x1, local copies, waits for them, and re-layouts, local(): both = jnp.concatenate([part_w.astype(BF16), small.astype(BF16)], axis=2)  12.6 us
    all_gather x1, blocking collectives, local(): pack = lax.all_gather(pack, 'segment', axis=0, tiled=True)  10.2 us
  transfers between devices with their start and end apart: 3, of which 3 were waited for; matrix products, arithmetic and copies ran while one was open for 1% of the time, Pallas kernels for 0%

profile of v1, /device:TPU:1, one launch (start us, length us, event | category | flops | bytes accessed | tf_op | source)
XLA Modules:
  0.0 446.0 jit_solution(16106216361713739180)
XLA Ops:
  7.2 0.0 all-gather.3.cloned.1.call-start
  7.2 3.1 constant_dynamic-slice_fusion
  10.3 0.0 all-gather.3.cloned.1.call-update
  10.4 0.0 copy-start.2
  10.4 0.0 copy-start.3
  10.4 0.0 all-gather.5.cloned.1.call-start
  10.4 86.1 %all-gather.3.cloned.1.call-done = bf16[8,512,1024]{2,1,0:T(8,128)(2,1)} async-done(((bf16[2,512,1024]{2,1,0:T(8,128)(2,1)}), bf16[8,512,1024]{2,1,0:T(8,128)(2,1)}) %all-gather.3.cloned.1.call-update) | async-done | bytes 8388624 | tf_op jit(solution)/shard_map/all_gather | solution.py:511
  96.6 0.0 all-gather.5.cloned.1.call-update
  96.6 0.0 all-reduce.4.cloned.1.call-start
  97.4 0.1 broadcast_in_dim.20
  97.5 0.1 broadcast_in_dim.21
  97.6 0.1 concatenate.6
  97.7 10.2 %all_gather.11 = f32[8,13,1024]{2,1,0:T(8,128)S(1)} all-gather(f32[2,13,1024]{2,1,0:T(8,128)S(1)} %concatenate.6), channel_id=1, replica_groups=mesh['dp'=2,'segment'=4,'rows'=16] {'segment'}, dimensions={0}, use_global_device_ids=true | all-gather | bytes 532480 | tf_op jit(solution)/shard_map/all_gather | solution.py:518
  107.9 0.8 reshape.42.par_ref
  108.7 0.7 slice_reduce_fusion
  109.4 1.8 dynamic-slice_bitcast_fusion
  111.1 21.5 %all-gather.5.cloned.1.call-done.w_hbm = bf16[8,1024,1024]{2,1,0:T(8,128)(2,1)} async-done(((bf16[8,512,1024]{2,1,0:T(8,128)(2,1)}), bf16[8,1024,1024]{2,1,0:T(8,128)(2,1)}) %all-gather.5.cloned.1.call-update) | async-done | bytes 16777232 | tf_op jit(solution)/shard_map/all_gather | solution.py:512
  132.6 164.4 %window.1 = (bf16[4,64,1024]{2,1,0:T(8,128)(2,1)}, bf16[2,4,64,1024]{3,2,1,0:T(8,128)(2,1)}, bf16[2,4,64,1024]{3,2,1,0:T(8,128)(2,1)}, f32[2,88,128]{2,1,0:T(8,128)}) custom-call(bf16[64,1024]{1,0:T(8,128)(2,1)} %get-tuple-element.27.x_ref, bf16[64,1024]{1,0:T(8,128)(2,1)} %get-tuple-element.26.cot_ref, ...), custom_call_target="tpu_custom_call" | custom-call | tf_op jit(solution)/shard_map/window/pallas_call | solution.py:449
  297.1 0.9 convert.6
  298.0 2.8 convolution_convert_fusion
  300.9 2.4 fusion.1
  303.3 12.6 %copy.22 = bf16[2,1024,1152]{2,0,1:T(2,128)(2,1)} copy(bf16[2,1024,1152]{1,2,0:T(8,128)(2,1)} %fusion.1) | data formatting | bytes 9437184 | tf_op jit(solution)/shard_map/concatenate | solution.py:528
  315.8 0.0 all-reduce.4.cloned.1.call-update
  315.8 0.6 copy-done.5
  316.5 0.6 dynamic-slice
  317.7 117.7 %all-reduce.4.cloned.1.call-done = bf16[2,1024,1152]{2,0,1:T(2,128)(2,1)} async-done(((bf16[2,1024,1152]{2,0,1:T(2,128)(2,1)}), bf16[2,1024,1152]{2,0,1:T(2,128)(2,1)}) %all-reduce.4.cloned.1.call-update) | async-done | bytes 4718608
  435.4 1.0 dynamic-slice_convert_fusion
  436.5 0.8 copy.23
  437.3 0.1 slice.34
  437.3 0.7 copy.25
  438.0 0.7 copy.24
  438.7 0.8 copy.30
  (17 shorter events, 0.2 us)
Async XLA Ops:
  7.2 89.4 %all-gather.3.cloned.1.call-start = ((), (), s32[]{:S(2)}) async-start(), calls=%async_computation | async-start | bytes 10485760 | tf_op jit(solution)/shard_map/all_gather | solution.py:511
  10.3 86.3 %copy-start.1 = (f32[2,9,1024]{2,0,1:T(2,128)S(1)}, f32[2,9,1024]{2,0,1:T(2,128)}, u32[]{:S(2)}) copy-start(f32[2,9,1024]{2,0,1:T(2,128)} %param.11) | copy-start | bytes 221188
  10.4 87.0 %copy-start.2 = (f32[2,1024]{1,0:T(2,128)S(1)}, f32[2,1024]{1,0:T(2,128)}, u32[]{:S(2)}) copy-start(f32[2,1024]{1,0:T(2,128)} %param.12) | copy-start | bytes 24580
  10.4 87.0 %copy-start.3 = (f32[2,1024]{1,0:T(2,128)S(1)}, f32[2,1024]{1,0:T(2,128)}, u32[]{:S(2)}) copy-start(f32[2,1024]{1,0:T(2,128)} %param.13) | copy-start | bytes 24580
  10.4 87.0 %copy-start.4 = (s32[2]{0:T(128)S(1)}, s32[2]{0:T(128)}, u32[]{:S(2)}) copy-start(s32[2]{0:T(128)} %param.15) | copy-start | bytes 28
  10.4 122.2 %all-gather.5.cloned.1.call-start = ((), (), s32[]{:S(2)}) async-start(), calls=%async_computation.1 | async-start | bytes 25165824 | tf_op jit(solution)/shard_map/all_gather | solution.py:512
  96.6 338.8 %all-reduce.4.cloned.1.call-start = ((), (), s32[]{:S(2)}) async-start(), calls=%async_computation.2 | async-start | bytes 9437184
  315.8 0.7 copy-start.5
  315.8 122.9 %copy-start = (bf16[4,64,1024]{2,1,0:T(8,128)(2,1)S(1)}, bf16[4,64,1024]{2,1,0:T(8,128)(2,1)}, u32[]{:S(2)}) copy-start(bf16[4,64,1024]{2,1,0:T(8,128)(2,1)} %get-tuple-element.8) | copy-start | bytes 1572868
Sparse Core Ops, SparseCore 0:
  10.5 86.0 all-gather.2
  98.2 34.3 all-gather.4
  316.0 119.3 all-reduce.3

commit v2 on v1

--- a/solution.py
+++ b/solution.py
@@ -27,8 +27,7 @@
     act_ref,
     dil_ref,
     sec_out,
-    hid_out,
-    grad_out,
+    weight_out,
     small_out,
     wv,
     xs,
@@ -45,26 +44,47 @@
     gph,
     coth,
     stat_own,
-    stat_in,
+    stat_mid,
+    near_in,
+    far_in,
     norms,
     small,
     sec_in,
     hid_in,
     grad_in,
     small_in,
+    twin_out,
+    twin_in,
+    half_sum,
+    share_in,
+    tiny,
+    tiny_in,
     w_sem,
-    stat_ss,
-    stat_rs,
+    near_ss,
+    near_rs,
+    far_ss,
+    far_rs,
+    twin_ss,
+    twin_rs,
+    share_ss,
+    share_rs,
+    tiny_ss,
+    tiny_rs,
     halo_ss,
     halo_rs,
     own_ss,
     own_rs,
     copy_sem,
 ):
-    slots, segs, row_devs, local_rows, cols, chans = geo
+    slots, segs, row_devs, local_rows, cols, chans, dps = geo
     per = slots // segs
     half = segs // MICRO
-    group = half * row_devs
+    ring = min(4, row_devs)
+    lines = row_devs // ring
+    far = half * lines
+    plane = dps * row_devs
+    piece = chans // plane
+    part = chans // dps
     pos = local_rows * cols
     groups = chans // LANES
     wide = cols + 2 * DMAX
@@ -73,30 +93,48 @@
     seg = lax.axis_index("segment")
     row = lax.axis_index("rows")
     micro = seg // half
-    gid = (seg % half) * row_devs + row
+    core = lax.axis_index("dp")
+    line = row // ring
+    place = row % ring
     up = (row + row_devs - 1) % row_devs
     down = (row + 1) % row_devs
     has_up = row > 0
     has_down = row < row_devs - 1
 
-    def peer(k):
-        other = (gid + k) % group
-        return {"segment": micro * half + other // row_devs, "rows": other % row_devs}
+    def near_peer(k):
+        return {"rows": line * ring + (place + k) % ring}
+
+    def far_peer(k):
+        other = ((seg % half) * lines + line + k) % far
+        return {"segment": micro * half + other // lines, "rows": other % lines * ring + place}
+
+    def plane_index(k):
+        return (core * row_devs + row + k) % plane
+
+    def plane_peer(k):
+        other = plane_index(k)
+        return {"dp": other // row_devs, "rows": other % row_devs}
 
     def greet(k, carry):
-        pl.semaphore_signal(barrier, inc=1, device_id=peer(k), device_id_type=MESH)
+        pl.semaphore_signal(barrier, inc=1, device_id=plane_peer(k), device_id_type=MESH)
         return carry
 
     for j in range(slots):
-        pltpu.make_async_copy(w_hbm.at[j], wv.at[j], w_sem.at[j]).start()
+        pltpu.make_async_copy(w_hbm.at[j // per, :, j % per], wv.at[j], w_sem.at[j]).start()
 
     barrier = pltpu.get_barrier_semaphore()
-    lax.fori_loop(1, group, greet, 0)
-    outside = segs - half
-    for k in range(outside):
-        other = (micro * half + half + k) % segs
-        pl.semaphore_signal(barrier, inc=1, device_id={"segment": other}, device_id_type=MESH)
-    pl.semaphore_wait(barrier, group - 1 + outside)
+    lax.fori_loop(1, plane, greet, 0)
+    for k in range(1, segs):
+        pl.semaphore_signal(
+            barrier, inc=1, device_id={"segment": (seg + k) % segs}, device_id_type=MESH)
+    for k in range(1, far):
+        if k % lines:
+            other = (((seg % half) * lines + line + k) % far) // lines
+
+            @pl.when(other != seg % half)
+            def _():
+                pl.semaphore_signal(barrier, inc=1, device_id=far_peer(k), device_id_type=MESH)
+    pl.semaphore_wait(barrier, plane - 1 + segs - 1 + (half - 1) * (lines - 1))
 
     def halo_sends(step, src, up_dst, down_dst):
         a = pltpu.make_async_remote_copy(
@@ -116,21 +154,46 @@
     def bwd_sends(j):
         return halo_sends(slots + j, gpn.at[j], gph.at[j, 1], gph.at[j, 0])
 
-    def stat_send(step, k):
-        return pltpu.make_async_remote_copy(
-            stat_own.at[step], stat_in.at[step, k - 1], stat_ss.at[step], stat_rs.at[step],
-            device_id=peer(k), device_id_type=MESH)
+    def near_send(step, k):
+        return pltpu.make_async_remote_copy(
+            stat_own.at[step], near_in.at[step, k - 1], near_ss.at[step], near_rs.at[step],
+            device_id=near_peer(k), device_id_type=MESH)
+
+    def far_send(step, k):
+        return pltpu.make_async_remote_copy(
+            stat_mid.at[step], far_in.at[step, k - 1], far_ss.at[step], far_rs.at[step],
+            device_id=far_peer(k), device_id_type=MESH)
+
+    def near_all(step):
+        return pltpu.make_async_remote_copy(
+            near_in.at[step], near_in.at[step], near_ss.at[step], near_rs.at[step],
+            device_id=near_peer(1), device_id_type=MESH)
+
+    def far_all(step):
+        return pltpu.make_async_remote_copy(
+            far_in.at[step], far_in.at[step], far_ss.at[step], far_rs.at[step],
+            device_id=far_peer(1), device_id_type=MESH)
 
     def push_stats(step):
-        def body(k, carry):
-            stat_send(step, k).start()
-            return carry
-        lax.fori_loop(1, group, body, 0)
-
-    def stats_whole(step):
-        return pltpu.make_async_remote_copy(
-            stat_in.at[step], stat_in.at[step], stat_ss.at[step], stat_rs.at[step],
-            device_id=peer(1), device_id_type=MESH)
+        for k in range(1, ring):
+            near_send(step, k).start()
+
+    def total_stats(step):
+        near_all(step).wait_recv()
+        mid = stat_own[step]
+        for k in range(ring - 1):
+            mid = mid + near_in[step, k]
+        stat_mid[step] = mid
+        for k in range(1, far):
+            far_send(step, k).start()
+        far_all(step).wait_recv()
+        for k in range(far - 1):
+            mid = mid + far_in[step, k]
+        return mid
+
+    def sent_stats(step):
+        near_all(step).wait_send()
+        far_all(step).wait_send()
 
     def to_owner(src, dst, slot, kind, owner):
         return pltpu.make_async_remote_copy(
@@ -240,8 +303,7 @@
         push_stats(j)
         for a in fwd_sends(j):
             a.start()
-        stats_whole(j).wait_recv()
-        total = jnp.sum(stat_in[j], axis=0) + stat_own[j]
+        total = total_stats(j)
         center = total[0:SUB] / population
         spread = total[SUB : 2 * SUB] / population - center * center
         scaling = lax.rsqrt(spread + EPSILON)
@@ -283,12 +345,12 @@
         for g in range(groups):
             hs[j, :, g * LANES : (g + 1) * LANES] = hpos[pl.ds(g, pos, stride=SUB), :].astype(BF16)
         give(*hid_args(j))
-        pltpu.make_async_copy(w_hbm.at[j], wv.at[j], w_sem.at[j]).wait()
+        pltpu.make_async_copy(w_hbm.at[j // per, :, j % per], wv.at[j], w_sem.at[j]).wait()
         step = chans // 4
         active = switch(act_ref, j, (pos, step))
         for n in range(4):
             cut = slice(n * step, (n + 1) * step)
-            mixed = jnp.dot(hs[j], wv[j, :, cut], preferred_element_type=F32)
+            mixed = jnp.dot(hs[j], wv[j, :, :, cut].reshape(chans, step), preferred_element_type=F32)
             old = xs[j, 1, :, cut].astype(F32)
             xs[j + 1, 1, :, cut] = jnp.where(active, old + mixed, old).astype(BF16)
 
@@ -320,7 +382,7 @@
         width = chans // 4
         for n in range(4):
             gh = lax.dot_general(
-                gnat[...], wv[j, n * width : (n + 1) * width, :],
+                gnat[...], wv[j].reshape(chans, chans)[n * width : (n + 1) * width],
                 (((1,), (1,)), ((), ())), preferred_element_type=F32)
             gh = gh.astype(BF16).astype(F32)
             for k in range(width // LANES):
@@ -371,8 +433,7 @@
 
         @pl.when(j > 0)
         def _():
-            stats_whole(step).wait_recv()
-            total = jnp.sum(stat_in[step], axis=0) + stat_own[step]
+            total = total_stats(step)
             mean_a = total[0:SUB] / population
             mean_b = total[SUB : 2 * SUB] / population
             for side in range(2):
@@ -403,7 +464,7 @@
         given(*small_args(j))
         for a in fwd_sends(j):
             a.wait_send()
-        stats_whole(j).wait_send()
+        sent_stats(j)
 
         @pl.when(j % per == per - 1)
         def _():
@@ -413,7 +474,7 @@
         def _():
             for a in bwd_sends(j):
                 a.wait_send()
-            stats_whole(slots + j).wait_send()
+            sent_stats(slots + j)
 
         return carry
 
@@ -430,16 +491,107 @@
         landed(small_in.at[k, pl.ds(1, segs - 1)], k, 2)
     landed(sec_in.at[pl.ds(1, segs - 1)], per - 1, 3)
     sec_out[...] = sec_in[...]
-    hid_out[...] = hid_in[...]
-    grad_out[...] = grad_in[...]
-    small_out[...] = jnp.sum(small_in[...], axis=1)
+
+    twin = {"dp": 1 - core}
+    block = min(LANES, part)
+
+    def outer(b, first):
+        lhs = hid_in[b, :, :, pl.ds(pl.multiple_of(first, block), block)].reshape(segs * pos, block)
+        return lax.dot_general(
+            lhs, grad_in[b].reshape(segs * pos, chans),
+            (((0,), (0,)), ((), ())), preferred_element_type=F32)
+
+    def twin_send(b):
+        return pltpu.make_async_remote_copy(
+            twin_out.at[b], twin_in.at[b], twin_ss.at[b], twin_rs.at[b],
+            device_id=twin, device_id_type=MESH)
+
+    def share_send(b, k):
+        other = (row + k) % row_devs
+        return pltpu.make_async_remote_copy(
+            half_sum.at[b, pl.ds(pl.multiple_of(other * piece, piece), piece)],
+            share_in.at[b, k - 1], share_ss.at[b], share_rs.at[b],
+            device_id={"rows": other}, device_id_type=MESH)
+
+    def share_all(b):
+        return pltpu.make_async_remote_copy(
+            share_in.at[b], share_in.at[b], share_ss.at[b], share_rs.at[b],
+            device_id={"rows": (row + 1) % row_devs}, device_id_type=MESH)
+
+    def tiny_send(k):
+        band = plane_index(k) * groups // plane
+        return pltpu.make_async_remote_copy(
+            tiny.at[band], tiny_in.at[k - 1], tiny_ss, tiny_rs,
+            device_id=plane_peer(k), device_id_type=MESH)
+
+    def tiny_all():
+        return pltpu.make_async_remote_copy(
+            tiny_in, tiny_in, tiny_ss, tiny_rs, device_id=plane_peer(1), device_id_type=MESH)
+
+    def theirs(b):
+        def body(n, carry):
+            rows = pl.ds(pl.multiple_of(n * block, block), block)
+            twin_out[b, rows, :] = outer(b, (1 - core) * part + n * block).astype(BF16)
+            return carry
+        lax.fori_loop(0, part // block, body, 0)
+        twin_send(b).start()
+
+    def ours(b):
+        twin_send(b).wait_recv()
+
+        def body(n, carry):
+            rows = pl.ds(pl.multiple_of(n * block, block), block)
+            value = outer(b, core * part + n * block) + twin_in[b, rows, :].astype(F32)
+            half_sum[b, rows, :] = value.astype(BF16)
+            return carry
+        lax.fori_loop(0, part // block, body, 0)
+
+        def push(k, carry):
+            share_send(b, k).start()
+            return carry
+        lax.fori_loop(1, row_devs, push, 0)
+
+    for b in range(per):
+        theirs(b)
+    rows = per * 11
+    for b in range(per):
+        total = jnp.sum(small_in[b], axis=0)
+        gppos[b * 11 * SUB : (b + 1) * 11 * SUB, :] = total
+    for g in range(groups):
+        tiny[g, 0:rows, :] = gppos[pl.ds(g, rows, stride=SUB), :].astype(BF16)
+        tiny[g, rows:, :] = jnp.zeros((32 - rows, LANES), BF16)
+
+    def push_tiny(k, carry):
+        tiny_send(k).start()
+        return carry
+
+    lax.fori_loop(1, plane, push_tiny, 0)
+    for b in range(per):
+        ours(b)
+    tiny_all().wait_recv()
+    small_out[...] = jnp.sum(tiny_in[...].astype(F32), axis=0) + tiny[
+        plane_index(0) * groups // plane].astype(F32)
+    for b in range(per):
+        share_all(b).wait_recv()
+        own = half_sum[b, pl.ds(pl.multiple_of(row * piece, piece), piece), :].astype(F32)
+        for k in range(row_devs - 1):
+            own = own + share_in[b, k].astype(F32)
+        weight_out[b] = own
+    for b in range(per):
+        twin_send(b).wait_send()
+        share_all(b).wait_send()
+    tiny_all().wait_send()
 
 
 def run_window(geo, x, cot, weights, params, active, dilations):
-    slots, segs, row_devs, local_rows, cols, chans = geo
+    slots, segs, row_devs, local_rows, cols, chans, dps = geo
     per = slots // segs
     pos = local_rows * cols
-    group = segs // MICRO * row_devs
+    ring = min(4, row_devs)
+    far = segs // MICRO * (row_devs // ring)
+    plane = dps * row_devs
+    piece = chans // plane
+    part = chans // dps
     wide = cols + 2 * DMAX
     ext = 3 * local_rows * wide * SUB
     vm = pltpu.VMEM
@@ -450,14 +602,13 @@
         functools.partial(window_kernel, geo),
         out_shape=(
             jax.ShapeDtypeStruct((segs, pos, chans), BF16),
-            jax.ShapeDtypeStruct((per, segs, pos, chans), BF16),
-            jax.ShapeDtypeStruct((per, segs, pos, chans), BF16),
-            jax.ShapeDtypeStruct((per, 11 * SUB, LANES), F32),
+            jax.ShapeDtypeStruct((per, piece, chans), F32),
+            jax.ShapeDtypeStruct((32, LANES), F32),
         ),
         in_specs=[vmem, vmem, pl.BlockSpec(memory_space=pl.ANY), vmem, smem, smem],
-        out_specs=(vmem,) * 4,
+        out_specs=(vmem,) * 3,
         scratch_shapes=[
-            vm((slots, chans, chans), BF16),
+            vm((slots, plane, piece, chans), BF16),
             vm((slots + 1, 3, pos, chans), BF16),
             vm((slots, 3 * pos * SUB, LANES), F32),
             vm((slots, ext, LANES), F32),
@@ -472,16 +623,32 @@
             vm((slots, 2, pos, chans), BF16),
             vm((2, pos, chans), BF16),
             vm((2 * slots, 2 * SUB, LANES), F32),
-            vm((2 * slots, group - 1, 2 * SUB, LANES), F32),
+            vm((2 * slots, 2 * SUB, LANES), F32),
+            vm((2 * slots, ring - 1, 2 * SUB, LANES), F32),
+            vm((2 * slots, far - 1, 2 * SUB, LANES), F32),
             vm((slots, 2 * SUB, LANES), F32),
             vm((slots, 11 * SUB, LANES), F32),
             vm((segs, pos, chans), BF16),
             vm((per, segs, pos, chans), BF16),
             vm((per, segs, pos, chans), BF16),
             vm((per, segs, 11 * SUB, LANES), F32),
+            vm((per, part, chans), BF16),
+            vm((per, part, chans), BF16),
+            vm((per, part, chans), BF16),
+            vm((per, row_devs - 1, piece, chans), BF16),
+            vm((chans // LANES, 32, LANES), BF16),
+            vm((plane - 1, 32, LANES), BF16),
             dma((slots,)),
             dma((2 * slots,)),
             dma((2 * slots,)),
+            dma((2 * slots,)),
+            dma((2 * slots,)),
+            dma((per,)),
+            dma((per,)),
+            dma((per,)),
+            dma((per,)),
+            dma,
+            dma,
             dma((2 * slots + 1, 2)),
             dma((2 * slots + 1, 2)),
             dma((slots, 4)),
@@ -503,13 +670,15 @@
     count, local_rows, cols, _ = images.shape
     slots = per * segs
     pos = local_rows * cols
-    geo = (slots, segs, row_devs, local_rows, cols, chans)
+    geo = (slots, segs, row_devs, local_rows, cols, chans, dps)
+    plane = dps * row_devs
+    piece = chans // plane
+    index = lax.axis_index("dp") * row_devs + lax.axis_index("rows")
     x = lax.dynamic_index_in_dim(images.reshape(count, pos, chans), seg, 0, keepdims=False)
     cot = lax.dynamic_index_in_dim(cotangent.reshape(count, pos, chans), seg, 0, keepdims=False)
-    part = chans // dps
-    mine = lax.dynamic_slice_in_dim(pointwise, lax.axis_index("dp") * part, part, 1)
-    weights = lax.all_gather(mine, "segment", axis=0, tiled=True)
-    weights = lax.all_gather(weights, "dp", axis=1, tiled=True)
+    mine = lax.dynamic_slice_in_dim(pointwise, index * piece, piece, 1)
+    weights = lax.all_gather(mine, ("segment", "dp", "rows"))
+    weights = weights.reshape(segs, plane, per, piece, chans)
     flags = (jnp.arange(per, dtype=jnp.int32) < cell_counts[0]).astype(F32)
     pack = jnp.concatenate(
         [depthwise, norm_gain[:, None], norm_shift[:, None],
@@ -519,18 +688,12 @@
     active = pack[:, 11, 0]
     rates = pack[:, 12, 0]
     params = pack[:, :11].reshape(slots, 11 * SUB, LANES)
-    sec, hid, grad, small = run_window(geo, x, cot, weights, params, active, rates)
-    hid = hid.reshape(per, segs * pos, chans)
-    grad = grad.reshape(per, segs * pos, chans)
-    part_w = lax.dot_general(hid, grad, (((1,), (1,)), ((0,), (0,))), preferred_element_type=F32)
-    small = jnp.swapaxes(small.reshape(per, 11, chans), 1, 2)
-    small = jnp.pad(small, ((0, 0), (0, 0), (0, LANES - 11)))
-    both = jnp.concatenate([part_w.astype(BF16), small.astype(BF16)], axis=2)
-    both = lax.psum_scatter(both, ("dp", "rows"), scatter_dimension=1, tiled=True).astype(F32)
-    grad_small = jnp.swapaxes(both[:, :, chans : chans + 11], 1, 2)
+    sec, grad_weight, small = run_window(geo, x, cot, weights, params, active, rates)
+    small = small[: per * 11].reshape(per, 11, LANES)
+    grad_small = lax.dynamic_slice_in_dim(small, index * piece % LANES, min(piece, LANES), 2)
     return (
         sec.reshape(1, count, local_rows, cols, chans),
-        both[:, :, :chans],
+        grad_weight,
         grad_small[:, :9],
         grad_small[:, 9:],
     )

time: 447 us -> 304 us (0.68)
  waiting for transfers between devices: 225 us -> 66.6 us
  Pallas kernels: 164 us -> 197 us
  local copies, waits for them, and re-layouts: 23.5 us -> 12.9 us
    unnamed x4 -> x1, waiting for transfers between devices: 118 us -> 0.02 us
    all_gather x2 -> x1, waiting for transfers between devices: 108 us -> 66.6 us  [local(): weights = lax.all_gather(mine, ('segment', 'dp', 'rows'))]
    pallas_call x1, Pallas kernels: 164 us -> 197 us  [run_window(): pl.pallas_call(functools.partial(window_kernel, geo), out_shape=(jax.Shap...]
    concatenate x1 -> x0, local copies, waits for them, and re-layouts: 12.6 us -> none  [local(): both = jnp.concatenate([part_w.astype(BF16), small.astype(BF16)], axis=2)]
  transfers between devices with their start and end apart: 3 -> 1, of which waited for: 3 -> 1; matrix products, arithmetic and copies ran while one was open for 1% -> 2% of each run, Pallas kernels for 0% -> 0%
where the time goes in v2:
time: 304 us
  Pallas kernels  197 us (65%)
  waiting for transfers between devices  66.6 us (22%)
  between operations  14.7 us (5%)
  local copies, waits for them, and re-layouts  12.9 us (4%)
  blocking collectives  12.3 us (4%)
    pallas_call x1, Pallas kernels, run_window(): pl.pallas_call(functools.partial(window_kernel, geo), out_shape=(jax.Shap...  197 us
    all_gather x1, waiting for transfers between devices, local(): weights = lax.all_gather(mine, ('segment', 'dp', 'rows'))  66.6 us
    all_gather x1, blocking collectives, local(): pack = lax.all_gather(pack, 'segment', axis=0, tiled=True)  12.3 us
  transfers between devices with their start and end apart: 1, of which 1 were waited for; matrix products, arithmetic and copies ran while one was open for 2% of the time, Pallas kernels for 0%

profile of v2, /device:TPU:1, one launch (start us, length us, event | category | flops | bytes accessed | tf_op | source)
XLA Modules:
  0.0 303.7 jit_solution(4558198879272409871)
XLA Ops:
  7.2 0.0 all-gather.3.cloned.1.call-start
  7.2 1.6 constant_dynamic-slice_fusion.2
  8.8 0.0 all-gather.3.cloned.1.call-update
  8.8 0.9 copy.16
  10.4 0.7 broadcast_in_dim.8
  11.1 0.7 broadcast_in_dim.9
  11.8 0.7 compare_convert_fusion
  12.5 0.1 broadcast_in_dim.20
  12.6 0.1 broadcast_in_dim.21
  12.6 0.1 concatenate.3
  12.7 12.3 %all_gather.11 = f32[8,13,1024]{2,1,0:T(8,128)S(1)} all-gather(f32[2,13,1024]{2,1,0:T(8,128)S(1)} %concatenate.3), channel_id=1, replica_groups=mesh['dp'=2,'segment'=4,'rows'=16] {'segment'}, dimensions={0}, use_global_device_ids=true | all-gather | bytes 532480 | tf_op jit(solution)/shard_map/all_gather | solution.py:687
  25.0 0.8 reshape.39.par_ref
  25.8 0.7 slice_reduce_fusion
  26.4 1.7 dynamic-slice_bitcast_fusion
  28.1 66.6 %all-gather.3.cloned.1.call-done = bf16[256,32,1024]{2,1,0:T(8,128)(2,1)} async-done(((bf16[2,32,1024]{2,1,0:T(8,128)(2,1)}), bf16[256,32,1024]{2,1,0:T(8,128)(2,1)}) %all-gather.3.cloned.1.call-update) | async-done | bytes 16777232 | tf_op jit(solution)/shard_map/all_gather | solution.py:680
  94.7 196.6 %window.1 = (bf16[4,64,1024]{2,1,0:T(8,128)(2,1)}, f32[2,32,1024]{2,1,0:T(8,128)}, f32[32,128]{1,0:T(8,128)}) custom-call(bf16[64,1024]{1,0:T(8,128)(2,1)} %get-tuple-element.25.x_ref, bf16[64,1024]{1,0:T(8,128)(2,1)} %get-tuple-element.24.cot_ref, bf16[4,32,2,32,1024]{4,3,2,1,0:T(8,128)(2,1)} %bitcast.11, f32[8,88,128]{2,1,0:T(8,128)} %reshape.39.par_ref, ...), custom_call_target="tpu_custom_call" | custom-call | tf_op jit(solution)/shard_map/window/pallas_call | solution.py:601
  291.3 0.7 slice.21
  292.0 0.1 constant_dynamic-slice_fusion
  292.1 0.6 copy.17
  292.7 0.7 constant_dynamic-slice_fusion.1
  293.3 1.9 copy.21
  295.2 1.7 copy.22
  (2 shorter events, 0.0 us)
Async XLA Ops:
  7.2 87.6 %all-gather.3.cloned.1.call-start = ((), (), s32[]{:S(2)}) async-start(), calls=%async_computation | async-start | bytes 16908288 | tf_op jit(solution)/shard_map/all_gather | solution.py:680
Sparse Core Ops, SparseCore 0:
  11.1 83.5 all-gather.2

commit v3 on v2

--- a/solution.py
+++ b/solution.py
@@ -20,12 +20,10 @@
 
 def window_kernel(
     geo,
-    x_ref,
-    cot_ref,
+    x_hbm,
+    cot_hbm,
     w_hbm,
-    par_ref,
-    act_ref,
-    dil_ref,
+    pack_ref,
     sec_out,
     weight_out,
     small_out,
@@ -59,6 +57,19 @@
     share_in,
     tiny,
     tiny_in,
+    par_ref,
+    cot_ref,
+    in_sem,
+    par_ss,
+    par_rs,
+    x_ss,
+    x_rs,
+    one_ss,
+    one_rs,
+    two_ss,
+    two_rs,
+    mate_ss,
+    mate_rs,
     w_sem,
     near_ss,
     near_rs,
@@ -119,8 +130,17 @@
         pl.semaphore_signal(barrier, inc=1, device_id=plane_peer(k), device_id_type=MESH)
         return carry
 
-    for j in range(slots):
-        pltpu.make_async_copy(w_hbm.at[j // per, :, j % per], wv.at[j], w_sem.at[j]).start()
+    def own_weight(b):
+        return pltpu.make_async_copy(w_hbm.at[b], wv.at[seg * per + b], w_sem.at[b])
+
+    inputs = (
+        pltpu.make_async_copy(x_hbm.at[seg], xs.at[0, 1], in_sem.at[0]),
+        pltpu.make_async_copy(cot_hbm.at[seg], cot_ref, in_sem.at[1]),
+    )
+    for copy in inputs:
+        copy.start()
+    for b in range(per):
+        own_weight(b).start()
 
     barrier = pltpu.get_barrier_semaphore()
     lax.fori_loop(1, plane, greet, 0)
@@ -178,7 +198,7 @@
         for k in range(1, ring):
             near_send(step, k).start()
 
-    def total_stats(step):
+    def total_stats(step, meanwhile=None):
         near_all(step).wait_recv()
         mid = stat_own[step]
         for k in range(ring - 1):
@@ -186,6 +206,8 @@
         stat_mid[step] = mid
         for k in range(1, far):
             far_send(step, k).start()
+        if meanwhile is not None:
+            meanwhile()
         far_all(step).wait_recv()
         for k in range(far - 1):
             mid = mid + far_in[step, k]
@@ -230,10 +252,158 @@
     def sec_args(j):
         return xs.at[j + 1, 1], sec_in.at[seg], j, 3, j // per
 
-    for a in cot_sends():
-        a.start()
-
-    xs[0, 1] = x_ref[...]
+    early = slots // 2
+    mine = core * row_devs + row
+    base = core * row_devs
+    mate = {"dp": 1 - core}
+
+    def away(j):
+        return (seg - j // per + segs) % segs
+
+    def remote(src, dst, ss, rs, j, where):
+        return pltpu.make_async_remote_copy(
+            src, dst, ss.at[j], rs.at[j], device_id=where, device_id_type=MESH)
+
+    def moved(ss, rs, j, count):
+        part_ref = wv.at[j, pl.ds(0, count)]
+        return remote(part_ref, part_ref, ss, rs, j, mate)
+
+    def half_ref(j):
+        return wv.at[j, pl.ds(base, row_devs)]
+
+    def place_peer(k):
+        return {"rows": line * ring + (place + k) % ring}
+
+    def line_peer(k):
+        return {"rows": (line + k) % lines * ring + place}
+
+    def first_count(j):
+        return (ring if j % 2 == 0 else lines) - 1
+
+    def second_count(j):
+        return row_devs - 1 - first_count(j)
+
+    def par_copy(k):
+        return remote(
+            pack_ref, par_ref.at[pl.ds(seg * per, per)], par_ss, par_rs, k - 1,
+            {"segment": (seg + k) % segs})
+
+    def seed(j):
+        @pl.when(away(j) == 0)
+        def _():
+            if j < early:
+                for k in range(1, segs):
+                    remote(w_hbm.at[j % per, mine], wv.at[j, mine], x_ss, x_rs, j,
+                           {"segment": (seg + k) % segs}).start()
+            else:
+                for k in (1, segs - 1):
+                    remote(w_hbm.at[j % per, pl.ds(base, row_devs)], half_ref(j), two_ss, two_rs, j,
+                           {"segment": (seg + k) % segs}).start()
+
+    def phase_one(j):
+        @pl.when(away(j) != 0)
+        def _():
+            moved(x_ss, x_rs, j, 1).wait_recv()
+            for k in range(1, first_count(j) + 1):
+                where = place_peer(k) if j % 2 == 0 else line_peer(k)
+                remote(wv.at[j, mine], wv.at[j, mine], one_ss, one_rs, j, where).start()
+
+    def phase_two(j):
+        @pl.when(away(j) != 0)
+        def _():
+            if first_count(j):
+                moved(one_ss, one_rs, j, first_count(j)).wait_recv()
+            if j % 2 == 0:
+                run = wv.at[j, pl.ds(base + line * ring, ring)]
+                for k in range(1, lines):
+                    remote(run, run, two_ss, two_rs, j, line_peer(k)).start()
+            else:
+                for k in range(1, ring):
+                    for n in range(lines):
+                        run = wv.at[j, base + n * ring + place]
+                        remote(run, run, two_ss, two_rs, j, place_peer(k)).start()
+
+    def to_mate(j):
+        remote(half_ref(j), half_ref(j), mate_ss, mate_rs, j, mate).start()
+
+    def relay(j):
+        cut = row_devs // 2
+        for near_seg, start, step in ((1, 0, 1), (segs - 1, cut, segs - 1)):
+            @pl.when(away(j) == near_seg)
+            def _():
+                moved(two_ss, two_rs, j, row_devs).wait_recv()
+                run = wv.at[j, pl.ds(base + start, cut)]
+                remote(run, run, two_ss, two_rs, j, {"segment": (seg + step) % segs}).start()
+                to_mate(j)
+
+    def complete(j):
+        if j < early:
+            @pl.when(away(j) != 0)
+            def _():
+                if second_count(j):
+                    moved(two_ss, two_rs, j, second_count(j)).wait_recv()
+                to_mate(j)
+        else:
+            @pl.when(away(j) == 2)
+            def _():
+                moved(two_ss, two_rs, j, row_devs).wait_recv()
+                to_mate(j)
+
+    def sent_weights(j):
+        @pl.when(away(j) == 0)
+        def _():
+            if j < early:
+                moved(x_ss, x_rs, j, segs - 1).wait_send()
+            else:
+                moved(two_ss, two_rs, j, 2 * row_devs).wait_send()
+
+        @pl.when(away(j) != 0)
+        def _():
+            moved(mate_ss, mate_rs, j, row_devs).wait_send()
+            if j < early:
+                if first_count(j):
+                    moved(one_ss, one_rs, j, first_count(j)).wait_send()
+                if second_count(j):
+                    moved(two_ss, two_rs, j, second_count(j)).wait_send()
+
+        if j >= early:
+            for near_seg in (1, segs - 1):
+                @pl.when(away(j) == near_seg)
+                def _():
+                    moved(two_ss, two_rs, j, row_devs // 2).wait_send()
+
+    def during(j):
+        for c in range(2, early):
+            @pl.when(j == c - 2)
+            def _():
+                phase_two(c)
+        for c in range(early, slots):
+            @pl.when(j == c - 3)
+            def _():
+                relay(c)
+
+        @pl.when(j == slots - 1)
+        def _():
+            for a in cot_sends():
+                a.start()
+
+    def after(j):
+        for c in range(1, slots):
+            @pl.when(j == c - 1)
+            def _():
+                complete(c)
+
+    for k in range(1, segs):
+        par_copy(k).start()
+    for c in range(slots):
+        seed(c)
+    par_ref[pl.ds(seg * per, per)] = pack_ref[...]
+    for c in range(early):
+        phase_one(c)
+    for c in range(2):
+        phase_two(c)
+    for copy in inputs:
+        copy.wait()
 
     edge = jnp.zeros((DMAX * SUB, LANES), F32)
 
@@ -287,8 +457,11 @@
                 found.append(jnp.where(two, both[1], both[0]) if len(both) > 1 else both[0])
         return found
 
-    def switch(ref, j, shape):
-        return jnp.full(shape, ref[j], F32) > 0.5
+    def switch(j, t):
+        return jnp.broadcast_to(param(j, t), (SUB, SUB, LANES)) > 0.5
+
+    def row_switch(j):
+        return jnp.broadcast_to(par_ref[j, 11 * SUB : 11 * SUB + 1, :], (pos, LANES)) > 0.5
 
     def forward(j, carry):
         spread_out(xs.at[j, 1], xpos.at[j], pos)
@@ -303,7 +476,15 @@
         push_stats(j)
         for a in fwd_sends(j):
             a.start()
-        total = total_stats(j)
+        total = total_stats(j, lambda: during(j))
+
+        @pl.when((j % per == 0) & (away(j) != 0))
+        def _():
+            first = pl.ds(j, per)
+            pltpu.make_async_remote_copy(
+                par_ref.at[first], par_ref.at[first], par_ss.at[0], par_rs.at[away(j) - 1],
+                device_id=mate, device_id_type=MESH).wait_recv()
+
         center = total[0:SUB] / population
         spread = total[SUB : 2 * SUB] / population - center * center
         scaling = lax.rsqrt(spread + EPSILON)
@@ -330,7 +511,7 @@
         for r in range(local_rows):
             activate(r)
             activate(2 * local_rows + r)
-        two = switch(dil_ref, j, (SUB, SUB, LANES))
+        two = switch(j, 12)
         taps = [param(j, t) for t in range(9)]
 
         def mix(chunk, carry):
@@ -345,14 +526,31 @@
         for g in range(groups):
             hs[j, :, g * LANES : (g + 1) * LANES] = hpos[pl.ds(g, pos, stride=SUB), :].astype(BF16)
         give(*hid_args(j))
-        pltpu.make_async_copy(w_hbm.at[j // per, :, j % per], wv.at[j], w_sem.at[j]).wait()
+
+        @pl.when(j == 0)
+        def _():
+            complete(0)
+
+        @pl.when(away(j) == 0)
+        def _():
+            own_weight(j % per).wait()
+
+        @pl.when(away(j) != 0)
+        def _():
+            moved(mate_ss, mate_rs, j, row_devs).wait_recv()
+
         step = chans // 4
-        active = switch(act_ref, j, (pos, step))
+        active = row_switch(j)
         for n in range(4):
-            cut = slice(n * step, (n + 1) * step)
-            mixed = jnp.dot(hs[j], wv[j, :, :, cut].reshape(chans, step), preferred_element_type=F32)
-            old = xs[j, 1, :, cut].astype(F32)
-            xs[j + 1, 1, :, cut] = jnp.where(active, old + mixed, old).astype(BF16)
+            mixed = jnp.dot(
+                hs[j], wv[j, :, :, n * step : (n + 1) * step].reshape(chans, step),
+                preferred_element_type=F32)
+            for k in range(step // LANES):
+                cut = slice(n * step + k * LANES, n * step + (k + 1) * LANES)
+                old = xs[j, 1, :, cut].astype(F32)
+                new = old + mixed[:, k * LANES : (k + 1) * LANES]
+                xs[j + 1, 1, :, cut] = jnp.where(active, new, old).astype(BF16)
+        after(j)
 
         @pl.when(j % per == per - 1)
         def _():
@@ -374,10 +572,12 @@
     def backward(t, carry):
         j = slots - 1 - t
         step = slots + j
-        active = switch(act_ref, j, (SUB, SUB, LANES))
-        live = switch(act_ref, j, (SUB, LANES))
-        gs[j] = jnp.where(
-            switch(act_ref, j, (pos, chans)), gnat[pos : 2 * pos, :].astype(F32), 0.0).astype(BF16)
+        active = switch(j, 11)
+        live = param(j, 11) > 0.5
+        use = row_switch(j)
+        for g in range(groups):
+            cut = slice(g * LANES, (g + 1) * LANES)
+            gs[j, :, cut] = jnp.where(use, gnat[pos : 2 * pos, cut].astype(F32), 0.0).astype(BF16)
         give(*grad_args(j))
         width = chans // 4
         for n in range(4):
@@ -390,7 +590,7 @@
                 for r in range(3 * local_rows):
                     ghpos[pl.ds((r * wide + DMAX) * SUB + g, cols, stride=SUB), :] = gh[
                         r * cols : (r + 1) * cols, k * LANES : (k + 1) * LANES]
-        two = switch(dil_ref, j, (SUB, SUB, LANES))
+        two = switch(j, 12)
         taps = [param(j, k) for k in range(9)]
         gain = param(j, 9)
         shift = param(j, 10)
@@ -481,6 +681,10 @@
     lax.fori_loop(0, slots, finish, 0)
     for a in cot_sends():
         a.wait_send()
+    for c in range(slots):
+        sent_weights(c)
+    for k in range(1, segs):
+        par_copy(k).wait_send()
 
     def landed(dst, slot, kind):
         to_owner(dst, dst, slot, kind, (seg + 1) % segs).wait_recv()
@@ -583,7 +787,7 @@
     tiny_all().wait_send()
 
 
-def run_window(geo, x, cot, weights, params, active, dilations):
+def run_window(geo, images, cotangents, weights, params):
     slots, segs, row_devs, local_rows, cols, chans, dps = geo
     per = slots // segs
     pos = local_rows * cols
@@ -597,7 +801,6 @@
     vm = pltpu.VMEM
     dma = pltpu.SemaphoreType.DMA
     vmem = pl.BlockSpec(memory_space=pltpu.VMEM)
-    smem = pl.BlockSpec(memory_space=pltpu.SMEM)
     return pl.pallas_call(
         functools.partial(window_kernel, geo),
         out_shape=(
@@ -605,7 +808,7 @@
             jax.ShapeDtypeStruct((per, piece, chans), F32),
             jax.ShapeDtypeStruct((32, LANES), F32),
         ),
-        in_specs=[vmem, vmem, pl.BlockSpec(memory_space=pl.ANY), vmem, smem, smem],
+        in_specs=[pl.BlockSpec(memory_space=pl.ANY)] * 3 + [vmem],
         out_specs=(vmem,) * 3,
         scratch_shapes=[
             vm((slots, plane, piece, chans), BF16),
@@ -638,7 +841,20 @@
             vm((per, row_devs - 1, piece, chans), BF16),
             vm((chans // LANES, 32, LANES), BF16),
             vm((plane - 1, 32, LANES), BF16),
+            vm((slots, 13 * SUB, LANES), F32),
+            vm((pos, chans), BF16),
+            dma((2,)),
+            dma((segs - 1,)),
+            dma((segs - 1,)),
             dma((slots,)),
+            dma((slots,)),
+            dma((slots,)),
+            dma((slots,)),
+            dma((slots,)),
+            dma((slots,)),
+            dma((slots,)),
+            dma((slots,)),
+            dma((per,)),
             dma((2 * slots,)),
             dma((2 * slots,)),
             dma((2 * slots,)),
@@ -658,14 +874,13 @@
         compiler_params=pltpu.CompilerParams(
             collective_id=0, has_side_effects=True, vmem_limit_bytes=64000 * 1024),
         name="window",
-    )(x, cot, weights, params, active, dilations)
+    )(images, cotangents, weights, params)
 
 
 def local(images, cotangent, pointwise, depthwise, norm_gain, norm_shift, cell_counts, dilations):
     segs = lax.axis_size("segment")
     row_devs = lax.axis_size("rows")
     dps = lax.axis_size("dp")
-    seg = lax.axis_index("segment")
     per, chans = pointwise.shape[0], pointwise.shape[2]
     count, local_rows, cols, _ = images.shape
     slots = per * segs
@@ -674,21 +889,14 @@
     plane = dps * row_devs
     piece = chans // plane
     index = lax.axis_index("dp") * row_devs + lax.axis_index("rows")
-    x = lax.dynamic_index_in_dim(images.reshape(count, pos, chans), seg, 0, keepdims=False)
-    cot = lax.dynamic_index_in_dim(cotangent.reshape(count, pos, chans), seg, 0, keepdims=False)
-    mine = lax.dynamic_slice_in_dim(pointwise, index * piece, piece, 1)
-    weights = lax.all_gather(mine, ("segment", "dp", "rows"))
-    weights = weights.reshape(segs, plane, per, piece, chans)
     flags = (jnp.arange(per, dtype=jnp.int32) < cell_counts[0]).astype(F32)
     pack = jnp.concatenate(
         [depthwise, norm_gain[:, None], norm_shift[:, None],
          jnp.broadcast_to(flags[:, None, None], (per, 1, chans)),
          jnp.broadcast_to((dilations > 1).astype(F32)[:, None, None], (per, 1, chans))], axis=1)
-    pack = lax.all_gather(pack, "segment", axis=0, tiled=True)
-    active = pack[:, 11, 0]
-    rates = pack[:, 12, 0]
-    params = pack[:, :11].reshape(slots, 11 * SUB, LANES)
-    sec, grad_weight, small = run_window(geo, x, cot, weights, params, active, rates)
+    sec, grad_weight, small = run_window(
+        geo, images.reshape(count, pos, chans), cotangent.reshape(count, pos, chans),
+        pointwise.reshape(per, plane, piece, chans), pack.reshape(per, 13 * SUB, LANES))
     small = small[: per * 11].reshape(per, 11, LANES)
     grad_small = lax.dynamic_slice_in_dim(small, index * piece % LANES, min(piece, LANES), 2)
     return (

time: 304 us -> 267 us (0.88)
  waiting for transfers between devices: 66.6 us -> 0 us
  Pallas kernels: 197 us -> 256 us
  between operations: 14.7 us -> 1.33 us
  blocking collectives: 12.3 us -> 0 us
  local copies, waits for them, and re-layouts: 12.9 us -> 8.74 us
    all_gather x1 -> x0, waiting for transfers between devices: 66.6 us -> none  [local(): weights = lax.all_gather(mine, ('segment', 'dp', 'rows'))]
    pallas_call x1, Pallas kernels: 197 us -> 256 us  [run_window(): pl.pallas_call(functools.partial(window_kernel, geo), out_shape=(jax.Shap...]
    all_gather x1 -> x0, blocking collectives: 12.3 us -> none  [local(): pack = lax.all_gather(pack, 'segment', axis=0, tiled=True)]
    unnamed x4 -> x7, local copies, waits for them, and re-layouts: 5.06 us -> 6.52 us
  transfers between devices with their start and end apart: 1 -> 0, of which waited for: 1 -> 0; matrix products, arithmetic and copies ran while one was open for 2% -> 0% of each run, Pallas kernels for 0% -> 0%
where the time goes in v3:
time: 267 us
  Pallas kernels  256 us (96%)
  local copies, waits for them, and re-layouts  8.74 us (3%)
    pallas_call x1, Pallas kernels, run_window(): pl.pallas_call(functools.partial(window_kernel, geo), out_shape=(jax.Shap...  256 us
    unnamed x7, local copies, waits for them, and re-layouts  6.52 us

profile of v3, /device:TPU:1, one launch (start us, length us, event | category | flops | bytes accessed | tf_op | source)
XLA Modules:
  0.0 266.6 jit_solution(6061924237301768578)
XLA Ops:
  0.6 0.9 constant_dynamic-update-slice_fusion.4
  1.5 0.7 constant_dynamic-update-slice_fusion.3
  2.2 0.7 constant_dynamic-update-slice_fusion.2
  3.6 0.1 constant_dynamic-update-slice_fusion.1
  3.7 0.7 compare_convert_fusion
  4.3 0.1 constant_dynamic-update-slice_fusion
  4.5 0.7 reshape.39.pack_ref
  5.1 255.8 %window.1 = (bf16[4,64,1024]{2,1,0:T(8,128)(2,1)}, f32[2,32,1024]{2,1,0:T(8,128)}, f32[32,128]{1,0:T(8,128)}) custom-call(bf16[4,64,1024]{2,1,0:T(8,128)(2,1)} %bitcast.12, bf16[4,64,1024]{2,1,0:T(8,128)(2,1)} %bitcast.13, bf16[2,32,32,1024]{3,2,1,0:T(8,128)(2,1)} %bitcast.10, f32[2,104,128]{2,1,0:T(8,128)} %reshape.39.pack_ref), custom_call_target="tpu_custom_call" | custom-call | tf_op jit(solution)/shard_map/window/pallas_call | solution.py:804
  261.0 0.7 slice.9
  261.7 0.1 constant_dynamic-slice_fusion
  261.8 0.6 copy.15
  262.4 0.7 constant_dynamic-slice_fusion.1
  263.0 1.9 copy.23
  264.9 1.7 copy.24
  (3 shorter events, 0.0 us)
